TPU v7x, 32 devices: a whole 2x2x4 slice. The times are simulated.
32 devices in a mesh: groups: 2 (over x), fsdp: 16 (over z, y, core).
Axes of the slice: x: 2, y: 2, z: 4, core: 2. Of those that a mesh axis runs over, the one named last changes fastest.
Arguments:
- obs_feat: bfloat16 [12288, 2048], P(('groups', 'fsdp')), parts along dimension 0, may hold values from -6 to 6
- reward: float32 [512, 24], P(('groups', 'fsdp')), parts along dimension 0, may hold values from -22 to 22
- value_old: float32 [512, 25], P(('groups', 'fsdp')), parts along dimension 0, may hold values from -6 to 6
- done: int32 [512, 24], P(('groups', 'fsdp')), parts along dimension 0, may hold values 0 or 1
- minibatch_perm: int32 [12288], P(('groups', 'fsdp')), parts along dimension 0, may hold values from 0 to 6143, as said below
- old_mean: bfloat16 [12288, 12], P(('groups', 'fsdp')), parts along dimension 0, may hold values from -6 to 6
- noise: bfloat16 [12288, 12], P(('groups', 'fsdp')), parts along dimension 0, may hold values from -6 to 6
- gain_in: float32 [2048], replicated, may hold values from 0.5 to 1.5
- out_weight: bfloat16 [2048, 2048], P('fsdp'), may hold values from -0.125 to 0.125
- head_weight: bfloat16 [2048, 13], replicated, may hold values from -0.125 to 0.125
- log_std: float32 [12], replicated, may hold values from 0.7 to 1.3
Outputs:
- hidden_out: bfloat16 [12288, 2048], P(('groups', 'fsdp')), parts along dimension 0
- grad_weight: float32 [4096, 2048], P(('groups', 'fsdp')), parts along dimension 0
- grad_head: float32 [4096, 13], P('groups'), parts along dimension 0
- grad_std: float32 [24], P('groups'), parts along dimension 0
There are 2 independent parts, one for each index of `groups`. A program takes and returns all parts, laid end to end along the dimension named above; an argument that names none is the same for every part. Nothing has to cross between parts.
Inputs may be any that keep to these rules, and one draw needn't show every extreme that they name: `minibatch_perm`: rows of one index of fsdp go 24 to each index of fsdp; the block of 384 minibatch positions of index j holds at positions j * 384 + s * 24 + c the rows from index s; a permutation of all rows.
All inputs are finite; a program needn't handle non-finite values. No bound on the sum of `done` on one device may be relied on, other than what follows from the above.
Results may differ from a plain program's by a relative error of at most 0.0095.
Values may be sent and summed in bfloat16 or wider, within the bound.
A program may use at most 128 MiB of HBM per device.

v0:
```python
import functools

import jax
import jax.numpy as jnp
from jax import lax
from jax.experimental import pallas as pl
from jax.experimental.pallas import tpu as pltpu
from jax.sharding import PartitionSpec as P

GAMMA = 0.99
LAMBDA_GAE = 0.95
CLIP_EPS = 0.2
NORM_EPS = 1e-05
MESH = pl.DeviceIdType.MESH
TILE = 512


def chip_at(pos, ring):
    half = ring // 2
    col = pos // half
    row = col * (ring - 1 - pos) + (1 - col) * pos
    return 2 * row + col


class Ring:
    def __init__(self, n):
        self.n = n
        self.me = lax.axis_index("fsdp")
        self.ring = n // 2
        self.core = lax.rem(self.me, 2)
        chip = self.me // 2
        col = lax.rem(chip, 2)
        row = chip // 2
        self.pos = col * (self.ring - 1 - row) + (1 - col) * row
        self.step = 1 - 2 * self.core
        self.sibling = self.me + self.step

    def device(self, ahead, core):
        pos = lax.rem(self.pos + ahead + self.ring, self.ring)
        return 2 * chip_at(pos, self.ring) + core

    def down(self):
        return self.device(self.step, self.core)


def enter(n, me):
    barrier = pltpu.get_barrier_semaphore()

    @pl.loop(1, n)
    def _(k):
        pl.semaphore_signal(
            barrier, inc=1, device_id={"fsdp": lax.rem(me + k, n)}, device_id_type=MESH
        )

    pl.semaphore_wait(barrier, n - 1)


def remote(src, dst, send, recv, device):
    return pltpu.make_async_remote_copy(
        src_ref=src,
        dst_ref=dst,
        send_sem=send,
        recv_sem=recv,
        device_id={"fsdp": device},
        device_id_type=MESH,
    )


def pieces(rows):
    count = 2 if rows % 32 == 0 else 1
    return [pl.ds(i * (rows // count), rows // count) for i in range(count)]


def spread(n, me, source_of, dst, send, recv):
    @pl.loop(1, n)
    def _(k):
        peer = lax.rem(me + k, n)
        remote(source_of(peer), dst.at[me], send, recv, peer).start()


def collect(n, slots, sem):
    part = slots.at[pl.ds(0, n - 1)]
    pltpu.make_async_copy(part, part, sem).wait()


def forward_kernel(
    n, x_ref, normed_ref, stat_ref, w_ref, hidden_ref, sums_ref,
    held, stats, local_sem, ring_send, ring_recv, sib_send, sib_recv, stat_send, stat_recv,
):
    r = Ring(n)
    me, last = r.me, r.ring - 1
    own = pltpu.make_async_copy(w_ref, held.at[me], local_sem)
    own.start()
    enter(n, me)
    cuts = pieces(held.shape[1])
    down = r.down()

    def ring_copy(owner, step, i):
        part = held.at[owner, cuts[i]]
        return remote(part, part, ring_send.at[step, i], ring_recv.at[step, i], down)

    def sib_copy(owner, step, i):
        part = held.at[owner, cuts[i]]
        return remote(part, part, sib_send.at[step, i], sib_recv.at[step, i], r.sibling)

    def mine(step):
        return r.device(-r.step * step, r.core)

    def theirs(step):
        return r.device(r.step * step, 1 - r.core)

    def add(owner):
        for j in range(0, hidden_ref.shape[1], TILE):
            cols = pl.ds(j, TILE)
            hidden_ref[:, cols] += jnp.dot(
                normed_ref[owner], held[owner, :, cols], preferred_element_type=jnp.float32
            )

    own.wait()
    for i in range(len(cuts)):
        ring_copy(me, 1, i).start()
        sib_copy(me, 0, i).start()
    spread(n, me, lambda peer: stat_ref, stats, stat_send, stat_recv)
    stats[me] = stat_ref[...]
    hidden_ref[...] = x_ref[...].astype(jnp.float32)

    def hop(step, _):
        owner = mine(step)
        for i in range(len(cuts)):
            ring_copy(owner, step, i).wait_recv()

            @pl.when(step < last)
            def _():
                ring_copy(owner, step + 1, i).start()

            sib_copy(owner, step, i).start()
            if i == 0:
                add(mine(step - 1))
        for i in range(len(cuts)):
            sib_copy(theirs(step - 1), step - 1, i).wait_recv()
        add(theirs(step - 1))
        return 0

    lax.fori_loop(1, r.ring, hop, 0)
    add(mine(last))
    for i in range(len(cuts)):
        sib_copy(theirs(last), last, i).wait_recv()
    add(theirs(last))
    collect(n, stats, stat_recv)
    sums_ref[...] = jnp.sum(stats[...], 0)
    collect(n, stats, stat_send)

    def drain(step, _):
        owner = mine(step)
        for i in range(len(cuts)):
            @pl.when(step < last)
            def _():
                ring_copy(owner, step + 1, i).wait_send()

            sib_copy(owner, step, i).wait_send()
        return 0

    lax.fori_loop(0, r.ring, drain, 0)


def forward(n, x, normed, stat, weight):
    rows, width = x.shape
    shard = weight.shape[0]
    blocks = normed.reshape(rows, n, shard).transpose(1, 0, 2)
    count = len(pieces(shard))
    vmem = pl.BlockSpec(memory_space=pltpu.VMEM)
    sems = pltpu.SemaphoreType.DMA
    return pl.pallas_call(
        functools.partial(forward_kernel, n),
        name="forward",
        out_shape=(
            jax.ShapeDtypeStruct((rows, width), jnp.float32),
            jax.ShapeDtypeStruct(stat.shape, jnp.float32),
        ),
        in_specs=[vmem, vmem, vmem, pl.BlockSpec(memory_space=pl.ANY)],
        out_specs=(vmem, vmem),
        scratch_shapes=[
            pltpu.VMEM((n, shard, width), jnp.bfloat16),
            pltpu.VMEM((n,) + stat.shape, jnp.float32),
            sems(()),
            sems((n // 2, count)),
            sems((n // 2, count)),
            sems((n // 2, count)),
            sems((n // 2, count)),
            sems(()),
            sems(()),
        ],
        compiler_params=pltpu.CompilerParams(
            collective_id=0, has_side_effects=True, vmem_limit_bytes=60 << 20
        ),
        cost_estimate=pl.CostEstimate(
            flops=2 * rows * width * width, bytes_accessed=16 * rows * width, transcendentals=0
        ),
    )(x, blocks, stat, weight)


def backward_kernel(
    n, normed_ref, ghid_ref, head_ref, grad_ref, heads_ref,
    own, sib_out, sib_in, ring_out, ring_in, head_in, head_sum, head_all,
    ring_send, ring_recv, sib_send, sib_recv, head_sems,
):
    r = Ring(n)
    me, last = r.me, r.ring - 1
    enter(n, me)
    width = grad_ref.shape[1]
    cuts = pieces(grad_ref.shape[0])
    down = r.down()

    def product(owner, cols):
        return lax.dot_general(
            normed_ref[owner],
            ghid_ref[:, cols],
            (((0,), (0,)), ((), ())),
            preferred_element_type=jnp.float32,
        )

    def ring_copy(step, i):
        return remote(
            ring_out.at[step, cuts[i]], ring_in.at[step, cuts[i]],
            ring_send.at[step, i], ring_recv.at[step, i], down,
        )

    def sib_copy(step):
        return remote(
            sib_out.at[step], sib_in.at[step], sib_send.at[step], sib_recv.at[step], r.sibling
        )

    def terms(step):
        theirs = r.device(-r.step * (last - step), 1 - r.core)
        for j in range(0, width, TILE):
            cols = pl.ds(j, TILE)
            sib_out[step, :, cols] = product(theirs, cols).astype(jnp.bfloat16)
        sib_copy(step).start()
        mine = r.device(r.step * (last - step), r.core)
        for j in range(0, width, TILE):
            cols = pl.ds(j, TILE)
            own[:, cols] = product(mine, cols)
        sib_copy(step).wait_recv()

    terms(0)
    for i, cut in enumerate(cuts):
        ring_out[0, cut] = (own[cut] + sib_in[0, cut].astype(jnp.float32)).astype(jnp.bfloat16)
        ring_copy(0, i).start()
    spread(n, me, lambda peer: head_ref.at[peer], head_in, head_sems.at[0], head_sems.at[1])
    head_in[me] = head_ref[me]
    collect(n, head_in, head_sems.at[1])
    head_sum[...] = jnp.sum(head_in[...], 0)
    head_all[me] = head_sum[...]
    spread(n, me, lambda peer: head_sum, head_all, head_sems.at[2], head_sems.at[3])

    def hop(step, _):
        terms(step)
        for i, cut in enumerate(cuts):
            ring_copy(step - 1, i).wait_recv()
            ring_out[step, cut] = (
                own[cut]
                + sib_in[step, cut].astype(jnp.float32)
                + ring_in[step - 1, cut].astype(jnp.float32)
            ).astype(jnp.bfloat16)
            ring_copy(step, i).start()
        return 0

    lax.fori_loop(1, last, hop, 0)
    terms(last)
    for i, cut in enumerate(cuts):
        ring_copy(last - 1, i).wait_recv()
        grad_ref[cut] = (
            own[cut]
            + sib_in[last, cut].astype(jnp.float32)
            + ring_in[last - 1, cut].astype(jnp.float32)
        )
    collect(n, head_all, head_sems.at[3])
    heads_ref[...] = head_all[...]
    collect(n, head_in, head_sems.at[0])
    collect(n, head_all, head_sems.at[2])

    def drain(step, _):
        sib_copy(step).wait_send()

        @pl.when(step < last)
        def _():
            for i in range(len(cuts)):
                ring_copy(step, i).wait_send()

        return 0

    lax.fori_loop(0, r.ring, drain, 0)


def backward(n, normed, ghid, head):
    rows, width = ghid.shape
    shard = normed.shape[1] // n
    blocks = normed.reshape(rows, n, shard).transpose(1, 0, 2)
    count = len(pieces(shard))
    ring = n // 2
    vmem = pl.BlockSpec(memory_space=pltpu.VMEM)
    sems = pltpu.SemaphoreType.DMA
    return pl.pallas_call(
        functools.partial(backward_kernel, n),
        name="backward",
        out_shape=(
            jax.ShapeDtypeStruct((shard, width), jnp.float32),
            jax.ShapeDtypeStruct(head.shape, jnp.float32),
        ),
        in_specs=[vmem, vmem, vmem],
        out_specs=(vmem, vmem),
        scratch_shapes=[
            pltpu.VMEM((shard, width), jnp.float32),
            pltpu.VMEM((ring, shard, width), jnp.bfloat16),
            pltpu.VMEM((ring, shard, width), jnp.bfloat16),
            pltpu.VMEM((ring - 1, shard, width), jnp.bfloat16),
            pltpu.VMEM((ring - 1, shard, width), jnp.bfloat16),
            pltpu.VMEM(head.shape, jnp.float32),
            pltpu.VMEM(head.shape[1:], jnp.float32),
            pltpu.VMEM(head.shape, jnp.float32),
            sems((ring - 1, count)),
            sems((ring - 1, count)),
            sems((ring,)),
            sems((ring,)),
            sems((4,)),
        ],
        compiler_params=pltpu.CompilerParams(
            collective_id=1, has_side_effects=True, vmem_limit_bytes=60 << 20
        ),
        cost_estimate=pl.CostEstimate(
            flops=2 * rows * width * width, bytes_accessed=32 * rows * width, transcendentals=0
        ),
    )(blocks, ghid, head)


def advantages(reward, value_old, done):
    keep = 1.0 - done.astype(jnp.float32)
    deltas = reward + GAMMA * value_old[:, 1:] * keep - value_old[:, :-1]

    def walk(carry, inputs):
        dstep, kstep = inputs
        carry = dstep + GAMMA * LAMBDA_GAE * kstep * carry
        return (carry, carry)

    start = jnp.zeros((reward.shape[0],), jnp.float32)
    _, stacked = lax.scan(walk, start, (deltas.T, keep.T), reverse=True)
    gae = stacked.T
    return (gae.reshape(-1), (gae + value_old[:, :-1]).reshape(-1))


def split3(value):
    first = lax.reduce_precision(value, 8, 7)
    second = lax.reduce_precision(value - first, 8, 7)
    third = value - first - second
    return [part.astype(jnp.bfloat16) for part in (first, second, third)]


def local(
    obs_feat,
    reward,
    value_old,
    done,
    minibatch_perm,
    old_mean,
    noise,
    gain_in,
    out_weight,
    head_weight,
    log_std,
):
    gae, returns = advantages(reward, value_old, done)
    local_rows, width = obs_feat.shape
    devices = lax.axis_size("fsdp")
    total_rows = local_rows * devices
    xf = obs_feat.astype(jnp.float32)
    normed = (xf * lax.rsqrt(jnp.mean(xf * xf, -1, keepdims=True) + NORM_EPS) * gain_in).astype(
        jnp.bfloat16
    )
    lane = lax.broadcasted_iota(jnp.int32, (8, 128), 1)
    stat = jnp.where(lane == 0, jnp.sum(gae), jnp.where(lane == 1, jnp.sum(gae * gae), 0.0))
    hidden, sums = forward(devices, obs_feat, normed, stat, out_weight)

    per_peer = local_rows // devices
    send_slot = minibatch_perm // local_rows * per_peer + minibatch_perm % per_peer
    place = (jnp.arange(local_rows)[:, None] == send_slot[None, :]).astype(jnp.bfloat16)
    send_hidden = jnp.dot(place, hidden.astype(jnp.bfloat16), preferred_element_type=jnp.bfloat16)
    hidden_out = lax.all_to_all(send_hidden, "fsdp", split_axis=0, concat_axis=0, tiled=True)

    mean_adv = sums[0, 0] / total_rows
    var_adv = sums[0, 1] / total_rows - mean_adv * mean_adv
    adv_b = ((gae - mean_adv) * lax.rsqrt(var_adv + NORM_EPS)).astype(jnp.bfloat16)
    ret_b = returns.astype(jnp.bfloat16)
    scale = 1.0 / jnp.sqrt(jnp.float32(total_rows))
    rinv = lax.rsqrt(jnp.mean(hidden * hidden, -1, keepdims=True) + NORM_EPS)
    hnorm = hidden * rinv
    hnorm_b = hnorm.astype(jnp.bfloat16)
    heads = jnp.dot(hnorm_b, head_weight, preferred_element_type=jnp.float32)
    nact = log_std.shape[0]
    mean_act = heads[:, :nact]
    value = heads[:, nact]
    std_dev = jnp.exp(log_std)
    offset = old_mean.astype(jnp.float32) - mean_act
    sample = noise.astype(jnp.float32)
    logr = jnp.sum(-sample * offset / std_dev - offset * offset / (2.0 * std_dev * std_dev), -1)
    ratio = jnp.exp(logr)
    advant = adv_b.astype(jnp.float32)
    clipped = jnp.clip(ratio, 1.0 - CLIP_EPS, 1.0 + CLIP_EPS)
    active = ratio * advant <= clipped * advant
    gratio = jnp.where(active, -scale * advant, 0.0)
    glogr = gratio * ratio
    gmean = glogr[:, None] * (sample / std_dev + offset / (std_dev * std_dev))
    gvalue = scale * (value - ret_b.astype(jnp.float32))
    std_local = jnp.sum(
        glogr[:, None] * (sample * offset / std_dev + offset * offset / (std_dev * std_dev)), 0
    )
    ghead = jnp.concatenate([gmean, gvalue[:, None]], 1)
    parts = split3(ghead)
    head_local = sum(
        lax.dot_general(part, hnorm_b, (((0,), (0,)), ((), ())), preferred_element_type=jnp.float32)
        for part in parts
    )
    ghn = sum(
        lax.dot_general(part, head_weight, (((1,), (1,)), ((), ())), preferred_element_type=jnp.float32)
        for part in parts
    )
    ghid = rinv * (ghn - hnorm * jnp.mean(ghn * hnorm, -1, keepdims=True))
    ghid_b = ghid.astype(jnp.bfloat16)

    share = width // devices
    block = jnp.zeros((devices, 16, share), jnp.float32)
    block = block.at[:, : nact + 1].set(head_local.reshape(nact + 1, devices, share).swapaxes(0, 1))
    block = block.at[:, nact + 1, :nact].set(std_local)
    grad_weight, heads_all = backward(devices, normed, ghid_b, block)
    grad_head = heads_all[:, : nact + 1].swapaxes(0, 1).reshape(nact + 1, width).T
    grad_std = heads_all[0, nact + 1, :nact]
    return (hidden_out, grad_weight, grad_head, grad_std)


def solution(mesh):
    return jax.shard_map(
        local,
        mesh=mesh,
        in_specs=(
            P(("groups", "fsdp"), None),
            P(("groups", "fsdp"), None),
            P(("groups", "fsdp"), None),
            P(("groups", "fsdp"), None),
            P(("groups", "fsdp")),
            P(("groups", "fsdp"), None),
            P(("groups", "fsdp"), None),
            P(),
            P("fsdp", None),
            P(),
            P(),
        ),
        out_specs=(
            P(("groups", "fsdp"), None),
            P(("groups", "fsdp"), None),
            P("groups", None),
            P("groups"),
        ),
        check_vma=False,
    )
```

profile of v0, /device:TPU:0, one launch (start us, length us, event | category | flops | bytes accessed | tf_op | source)
XLA Modules:
  0.0 166.6 jit_solution(7542560466267232586)
XLA Ops:
  0.7 0.9 fusion.23
  1.7 1.8 %while.19 = (s32[]{:T(128)}, f32[16]{0:T(128)S(1)}, f32[24,16]{1,0:T(8,128)S(1)}, f32[24,16]{1,0:T(8,128)S(1)}, f32[24,16]{1,0:T(8,128)S(1)}, /*index=5*/s32[]{:T(128)}, s32[]{:T(128)}, s32[]{:T(128)}) while((s32[]{:T(128)}, f32[16]{0:T(128)S(1)}, f32[24,16]{1,0:T(8,128)S(1)}, f32[24,16]{1,0:T(8,128)S(1)}, f32[24,16]{1,0:T(8,128)S(1)}, ...), condition=%wide.region_2.3_spmd.clone, body=%wide.region_1.2_spmd.clone.sunk | while | flops 68 | bytes 499 | solution.py:346
  3.5 0.6 reduce_sum.64
  4.2 0.6 fusion.19
  4.8 0.6 compare_select_fusion
  5.4 1.9 %copy.30 = bf16[384,2048]{0,1:T(8,128)(2,1)S(1)} copy(bf16[384,2048]{1,0:T(8,128)(2,1)} %x_ref.1) | data formatting | bytes 3145728 | tf_op args[0]
  8.2 1.6 copy.31
  9.8 1.2 broadcast_select_fusion.1.stat_ref
  11.0 53.7 %forward.1 = (f32[384,2048]{1,0:T(8,128)}, f32[8,128]{1,0:T(8,128)}) custom-call(bf16[384,2048]{1,0:T(8,128)(2,1)} %x_ref.1, bf16[16,384,128]{2,1,0:T(8,128)(2,1)} %bitcast.62, f32[8,128]{1,0:T(8,128)} %broadcast_select_fusion.1.stat_ref, bf16[128,2048]{1,0:T(8,128)(2,1)} %w_ref.1), custom_call_target="tpu_custom_call" | custom-call | flops 3221225472 | bytes 12582912 | tf_op jit(solution)/shard_map/forward/pallas_call | solution.py:173
  64.8 4.2 %fusion.5 = bf16[384,2048]{1,0:T(8,128)(2,1)} fusion(f32[384,2048]{1,0:T(8,128)} %get-tuple-element.136, s32[384]{0:T(512)S(1)} %fusion.26), kind=kOutput, calls=%fused_computation.15 | convolution fusion | flops 604913664 | bytes 4720128 | tf_op jit(solution)/shard_map/dot_general | solution.py:386
  69.0 4.7 %all-to-all-start = ((bf16[16,24,2048]{2,1,0:T(8,128)(2,1)}), bf16[16,24,2048]{2,1,0:T(8,128)(2,1)}, u32[]{:S(2)}, u32[]{:S(2)}) async-start(bf16[16,24,2048]{2,1,0:T(8,128)(2,1)} %bitcast.60), calls=%async_computation | async-start | bytes 3145728 | tf_op jit(solution)/shard_map/all_to_all | solution.py:387
  74.0 1.3 fusion.34
  78.1 1.4 multiply_convert_fusion.1
  79.6 2.0 %fusion.36 = f32[384,13]{0,1:T(8,128)S(1)} fusion(bf16[384,2048]{1,0:T(8,128)(2,1)} %multiply_convert_fusion.1, bf16[2048,13]{0,1:T(8,128)(2,1)S(1)} %copy-done), kind=kOutput, calls=%fused_computation.78 | convolution fusion | flops 20447232 | bytes 1646080 | tf_op jit(solution)/shard_map/dot_general | solution.py:397
  82.0 1.7 %fusion.29 = f32[13,2048]{1,0:T(8,128)S(1)} fusion(bf16[384,2048]{1,0:T(8,128)(2,1)} %multiply_convert_fusion.1, f32[384,1]{0,1:T(1,128)S(1)} %fusion.28, f32[384,12]{0,1:T(8,128)S(1)} %get-tuple-element.174), kind=kOutput, calls=%fused_computation.72 | convolution fusion | flops 20462208 | bytes 1699328 | tf_op jit(solution)/shard_map/dot_general | solution.py:419
  84.9 0.6 fusion.31
  86.1 1.2 multiply_reduce_fusion
  87.3 1.7 %multiply_convert_fusion.ghid_ref = bf16[384,2048]{1,0:T(8,128)(2,1)} fusion(f32[384,2048]{1,0:T(8,128)S(1)} %get-tuple-element.185, f32[384,2048]{1,0:T(8,128)S(1)} %copy-done.1, f32[384]{0:T(512)S(1)} %broadcast_multiply_fusion, f32[384]{0:T(512)S(1)} %add_rsqrt_fusion), kind=kLoop, calls=%fused_computation.8 | loop fusion | flops 3932160 | bytes 7867392 | tf_op jit(solution)/shard_map/convert_element_type | solution.py:427
  89.1 70.8 %backward.1 = (f32[128,2048]{1,0:T(8,128)}, f32[16,16,128]{2,1,0:T(8,128)}) custom-call(bf16[16,384,128]{2,1,0:T(8,128)(2,1)} %bitcast.63, bf16[384,2048]{1,0:T(8,128)(2,1)} %multiply_convert_fusion.ghid_ref, f32[16,16,128]{2,1,0:T(8,128)} %copy-done.4), custom_call_target="tpu_custom_call" | custom-call | flops 3221225472 | bytes 25165824 | tf_op jit(solution)/shard_map/backward/pallas_call | solution.py:303
  159.9 1.0 slice_bitcast_fusion
  161.0 0.7 copy.38
  161.7 1.2 slice_bitcast_fusion.1
  162.9 2.7 %copy.54 = bf16[384,2048]{1,0:T(8,128)(2,1)} copy(bf16[384,2048]{1,0:T(8,128)(2,1)} %bitcast.6) | data formatting | bytes 3145728
  165.6 1.0 copy.55
  (103 shorter events, 5.1 us)
Async XLA Ops:
  0.6 78.9 %copy-start = (bf16[2048,13]{0,1:T(8,128)(2,1)S(1)}, bf16[2048,13]{0,1:T(8,128)(2,1)}, u32[]{:S(2)}) copy-start(bf16[2048,13]{0,1:T(8,128)(2,1)} %param.26) | copy-start | bytes 159748
  0.6 7.1 %copy-start.8 = (f32[2048]{0:T(1024)S(1)}, f32[2048]{0:T(1024)}, u32[]{:S(2)}) copy-start(f32[2048]{0:T(1024)} %param.24) | copy-start | bytes 24580
  7.7 2.1 %copy-start.9 = (s32[384]{0:T(512)S(1)}, s32[384]{0:T(512)}, u32[]{:S(2)}) copy-start(s32[384]{0:T(512)} %param.21) | copy-start | bytes 4612
  64.8 8.9 %copy-start.1 = (f32[384,2048]{1,0:T(8,128)S(1)}, f32[384,2048]{1,0:T(8,128)}, u32[]{:S(2)}) copy-start(f32[384,2048]{1,0:T(8,128)} %get-tuple-element.136) | copy-start | bytes 9437188
  69.0 9.0 %copy-start.5 = (f32[16,25]{1,0:T(8,128)S(1)}, f32[16,25]{1,0:T(8,128)}, u32[]{:S(2)}) copy-start(f32[16,25]{1,0:T(8,128)} %param.19) | copy-start | bytes 4804
  69.0 93.9 %all-to-all-start = ((bf16[16,24,2048]{2,1,0:T(8,128)(2,1)}), bf16[16,24,2048]{2,1,0:T(8,128)(2,1)}, u32[]{:S(2)}, u32[]{:S(2)}) async-start(bf16[16,24,2048]{2,1,0:T(8,128)(2,1)} %bitcast.60), calls=%async_computation | async-start | bytes 3145728 | tf_op jit(solution)/shard_map/all_to_all | solution.py:387
  74.0 5.5 %copy-start.10 = (f32[12]{0:T(128)S(1)}, f32[12]{0:T(128)}, u32[]{:S(2)}) copy-start(f32[12]{0:T(128)} %param.27) | copy-start | bytes 148
  78.0 3.6 %copy-start.6 = (bf16[384,12]{0,1:T(8,128)(2,1)S(1)}, bf16[384,12]{0,1:T(8,128)(2,1)}, u32[]{:S(2)}) copy-start(bf16[384,12]{0,1:T(8,128)(2,1)} %param.23) | copy-start | bytes 27652
  78.0 3.6 %copy-start.7 = (bf16[384,12]{0,1:T(8,128)(2,1)S(1)}, bf16[384,12]{0,1:T(8,128)(2,1)}, u32[]{:S(2)}) copy-start(bf16[384,12]{0,1:T(8,128)(2,1)} %param.22) | copy-start | bytes 27652
  79.6 4.1 %copy-start.2 = (bf16[384,2048]{1,0:T(8,128)(2,1)S(1)}, bf16[384,2048]{1,0:T(8,128)(2,1)}, u32[]{:S(2)}) copy-start(bf16[384,2048]{1,0:T(8,128)(2,1)} %multiply_convert_fusion.1) | copy-start | bytes 4718596
  84.9 1.2 copy-start.4
  159.9 5.7 %copy-start.3 = (f32[128,2048]{1,0:T(8,128)S(1)}, f32[128,2048]{1,0:T(8,128)}, u32[]{:S(2)}) copy-start(f32[128,2048]{1,0:T(8,128)} %get-tuple-element.246) | copy-start | bytes 3145732
where the time goes:
time: 167 us
  Pallas kernels  125 us (75%)
  local copies, waits for them, and re-layouts  13.3 us (8%)
  matrix products  11 us (7%)
  other arithmetic  9.06 us (5%)
  starting transfers between devices  4.71 us (3%)
  between operations  3.56 us (2%)
    pallas_call x1, Pallas kernels, backward(): pl.pallas_call(functools.partial(backward_kernel, n), name='backward', ou...  70.8 us
    pallas_call x1, Pallas kernels, forward(): pl.pallas_call(functools.partial(forward_kernel, n), name='forward', out_...  53.7 us
    unnamed x30, local copies, waits for them, and re-layouts  6.51 us
    all_to_all x1, starting transfers between devices, local(): lax.all_to_all(send_hidden, 'fsdp', split_axis=0, concat_axis=0, tiled=True)  4.71 us
    dot_general x1, matrix products, local(): jnp.dot(place, hidden.astype(jnp.bfloat16), preferred_element_type=jnp.bf...  4.19 us
  transfers between devices with their start and end apart: 1, of which 0 were waited for; matrix products, arithmetic and copies ran while one was open for 9% of the time, Pallas kernels for 43%

commit v1 on v0

v1 whole, which is shorter than its diff:
```python
import functools

import jax
import jax.numpy as jnp
from jax import lax
from jax.experimental import pallas as pl
from jax.experimental.pallas import tpu as pltpu
from jax.sharding import PartitionSpec as P

GAMMA = 0.99
LAMBDA_GAE = 0.95
CLIP_EPS = 0.2
NORM_EPS = 1e-05
MESH = pl.DeviceIdType.MESH
LANES = 128
F32 = jnp.float32
BF16 = jnp.bfloat16


def chip_at(pos, ring):
    half = ring // 2
    col = pos // half
    row = col * (ring - 1 - pos) + (1 - col) * pos
    return 2 * row + col


class Place:
    def __init__(self, n):
        self.n = n
        self.me = lax.axis_index("fsdp")
        self.group = lax.axis_index("groups")
        self.ring = n // 2
        self.rows = n // 4
        self.core = lax.rem(self.me, 2)
        chip = self.me // 2
        self.col = lax.rem(chip, 2)
        self.row = chip // 2
        self.pos = self.col * (self.ring - 1 - self.row) + (1 - self.col) * self.row
        self.step = 1 - 2 * self.core
        self.sibling = self.me + self.step

    def on_ring(self, ahead, core):
        pos = lax.rem(self.pos + ahead + self.ring, self.ring)
        return 2 * chip_at(pos, self.ring) + core

    def at(self, row, col, core):
        return (row * 2 + col) * 2 + core


def remote(src, dst, send, recv, device):
    return pltpu.make_async_remote_copy(
        src_ref=src, dst_ref=dst, send_sem=send, recv_sem=recv, device_id=device, device_id_type=MESH
    )


def await_bytes(part, sem):
    pltpu.make_async_copy(part, part, sem).wait()


def halves(start, size):
    first = (size // LANES + 1) // 2 * LANES
    return [(start, first), (start + first, size - first)]


def lanes(start, size):
    return pl.ds(pl.multiple_of(start, LANES), size)


def kernel(
    n, steps,
    x_hbm, w_hbm, gain_ref, reward_ref, value_ref, done_ref, perm_ref, mean_ref, noise_ref, head_ref, std_ref,
    hid_ref, grad_ref, headg_ref, stdg_ref,
    xv, held, normed, hidden, hnorm, ghid, place, send, rows_t, cols, envs, head, lstd,
    stats, stat_own, head_blk, head_in, head_sum, head_all,
    sib_out, sib_in, y_out, y_in, z_out, z_in, own, prod,
    load_sems, ring_send, ring_recv, x_send, x_recv, sibr_recv, sibx_recv, sib_send,
    stat_send, stat_recv, a2a_send, a2a_recv, head_sems,
    rs_sib_send, rs_sib_recv, y_send, y_recv, z_send, z_recv,
):
    p = Place(n)
    me, last, L = p.me, p.ring - 1, p.rows
    rows, width = xv.shape
    shard = w_hbm.shape[0]
    block = normed.shape[2]
    whole_blocks = shard == block
    nact = mean_ref.shape[0]
    n_env = reward_ref.shape[0]
    slot_rows = send.shape[1]
    per = rows // n
    tile = width // 4
    tiles = [pl.ds(j * tile, tile) for j in range(4)]
    total_rows = rows * n

    load_x = pltpu.make_async_copy(x_hbm, xv, load_sems.at[0])
    load_x.start()
    load_w = pltpu.make_async_copy(w_hbm, held.at[pl.ds(pl.multiple_of(me * shard, shard), shard)], load_sems.at[1])
    load_w.start()

    barrier = pltpu.get_barrier_semaphore()

    @pl.loop(1, n)
    def _(k):
        pl.semaphore_signal(barrier, inc=1, device_id={"fsdp": lax.rem(me + k, n)}, device_id_type=MESH)

    pl.semaphore_signal(barrier, inc=1, device_id={"groups": 1 - p.group}, device_id_type=MESH)
    pl.semaphore_wait(barrier, n)

    xw = width // LANES * 5 // 16 * LANES
    rest = width - 2 * xw
    ring_cuts = halves(p.group * (width - xw), xw) + halves(xw, rest)
    x_cuts = halves((1 - p.group) * (width - xw), xw)
    next_chip = {"fsdp": p.on_ring(p.step, p.core)}
    sibling = {"fsdp": p.sibling}
    partner = {"groups": 1 - p.group}

    def part(owner, cut):
        return held.at[pl.ds(pl.multiple_of(owner * shard, shard), shard), lanes(*cut)]

    def ring_copy(owner, s, i):
        ref = part(owner, ring_cuts[i])
        return remote(ref, ref, ring_send, ring_recv.at[s, i], next_chip)

    def x_copy(owner, s, i):
        ref = part(owner, ring_cuts[i])
        return remote(ref, ref, x_send, x_recv.at[s, i], partner)

    def x_arrival(owner, s, i):
        ref = part(owner, x_cuts[i])
        return remote(ref, ref, x_send, x_recv.at[s, i], partner)

    def sibr_copy(owner, s, i):
        ref = part(owner, ring_cuts[i])
        return remote(ref, ref, sib_send, sibr_recv.at[s, i], sibling)

    def sibx_copy(owner, s, i):
        ref = part(owner, x_cuts[i])
        return remote(ref, ref, sib_send, sibx_recv.at[s, i], sibling)

    def mine(s):
        return p.on_ring(-p.step * s, p.core)

    def theirs(s):
        return p.on_ring(p.step * s, 1 - p.core)

    load_w.wait()
    for i in range(4):
        ring_copy(me, 1, i).start()
    for i in range(4):
        sibr_copy(me, 0, i).start()
    for i in range(2):
        sibx_copy(me, 0, i).start()

    load_x.wait()
    square = jnp.zeros((rows, LANES), F32)
    for j in range(0, width, LANES):
        xf = xv[:, j : j + LANES].astype(F32)
        square = square + xf * xf
    scale_x = lax.rsqrt(jnp.sum(square, -1, keepdims=True) / width + NORM_EPS)
    for j in range(width // block):
        at = pl.ds(j * block, block)
        xf = xv[:, at].astype(F32)
        hidden[:, at] = xf
        normed[j] = (xf * scale_x * gain_ref[:, at]).astype(BF16)

    def add(index):
        for cut in tiles:
            hidden[:, cut] += jnp.dot(
                normed[index], held[pl.ds(pl.multiple_of(index * block, block), block), cut],
                preferred_element_type=F32,
            )

    def add_shard(owner):
        if whole_blocks:
            add(owner)

    def spread(count, source_of, dst, send_sem, recv_sem):
        @pl.loop(1, n)
        def _(k):
            peer = lax.rem(me + k, n)

            def go():
                remote(source_of(peer), dst.at[me], send_sem, recv_sem, {"fsdp": peer}).start()

            if count == n:
                go()
            else:
                pl.when(peer < count)(go)

    def advantages():
        lane = lax.broadcasted_iota(jnp.int32, (n_env, LANES), 1)
        envs[...] = jnp.zeros_like(envs)
        envs[0, :, 0:steps] = reward_ref[...]
        envs[1, :, 0 : steps + 1] = value_ref[...]
        envs[2, :, 0:steps] = 1.0 - done_ref[...].astype(F32)
        value, keep = envs[1], envs[2]
        ahead = pltpu.roll(value, LANES - 1, 1)
        gae = jnp.where(lane < steps, envs[0] + GAMMA * ahead * keep - value, 0.0)
        decay = GAMMA * LAMBDA_GAE * keep
        shift = 1
        while shift < steps:
            gae = gae + decay * pltpu.roll(gae, LANES - shift, 1)
            decay = decay * pltpu.roll(decay, LANES - shift, 1)
            shift *= 2
        envs[0] = gae
        envs[3] = gae + value
        spot = lax.broadcasted_iota(jnp.int32, (8, LANES), 1)
        stat_own[...] = jnp.where(spot == 0, jnp.sum(gae), jnp.where(spot == 1, jnp.sum(gae * gae), 0.0))
        stats[me] = stat_own[...]
        spread(n, lambda peer: stat_own, stats, stat_send, stat_recv)
        at_step = lax.broadcasted_iota(jnp.int32, (steps, LANES), 0) == lax.broadcasted_iota(
            jnp.int32, (steps, LANES), 1
        )
        for e in range(n_env):
            for c, k in ((0, 0), (1, 3)):
                line = jnp.broadcast_to(envs[k, e : e + 1, :], (steps, LANES))
                cols[c, e * steps : (e + 1) * steps, :] = jnp.broadcast_to(
                    jnp.sum(jnp.where(at_step, line, 0.0), -1, keepdims=True), (steps, LANES)
                )

    def placement():
        perm = perm_ref[...]
        to = lax.div(perm, rows)
        slot = to * slot_rows + lax.rem(perm, per)
        place[...] = jnp.where(
            lax.broadcasted_iota(jnp.int32, place.shape, 0) == slot, 1.0, 0.0
        ).astype(BF16)

    def columns():
        for k, ref in ((0, mean_ref), (1, noise_ref)):
            rows_t[...] = jnp.zeros_like(rows_t)
            rows_t[0:nact] = ref[...].astype(F32)
            rows_t[16 : 16 + nact] = ref[...].astype(F32)
            cols[2 + k] = jnp.transpose(rows_t[...])
        head[...] = jnp.zeros_like(head)
        hf = head_ref[...].astype(F32)
        head[0 : nact + 1] = hf
        head[16 : 17 + nact] = hf
        lstd[...] = jnp.zeros_like(lstd)
        lstd[0:1, 0:nact] = std_ref[...]
        lstd[0:1, 16 : 16 + nact] = std_ref[...]

    def hop(s, _):
        owner = mine(s)
        for i in range(4):
            ring_copy(owner, s, i).wait_recv()

            @pl.when(s < last)
            def _():
                ring_copy(owner, s + 1, i).start()

            if i < 2:
                x_copy(owner, s, i).start()
            sibr_copy(owner, s, i).start()
        before = mine(s - 1)

        @pl.when(s > 1)
        def _():
            for i in range(2):
                x_arrival(before, s - 1, i).wait_recv()
                sibx_copy(before, s - 1, i).start()

        add_shard(before)

        @pl.when(s == 1)
        def _():
            advantages()

        @pl.when(s == 2)
        def _():
            placement()

        @pl.when(s == 3)
        def _():
            columns()

        @pl.when(s > 1)
        def _():
            other = theirs(s - 2)
            for i in range(4):
                sibr_copy(other, s - 2, i).wait_recv()
            for i in range(2):
                sibx_copy(other, s - 2, i).wait_recv()
            add_shard(other)

        return 0

    lax.fori_loop(1, p.ring, hop, 0)
    for i in range(2):
        x_arrival(mine(last), last, i).wait_recv()
        sibx_copy(mine(last), last, i).start()
    for s in (last - 1, last):
        other = theirs(s)
        if s == last:
            add_shard(mine(last))
        for i in range(4):
            sibr_copy(other, s, i).wait_recv()
        for i in range(2):
            sibx_copy(other, s, i).wait_recv()
        if s < last:
            add_shard(other)
    if not whole_blocks:
        lax.fori_loop(0, width // block - 1, lambda b, _: (add(b), 0)[1], 0)
    final = theirs(last) if whole_blocks else width // block - 1

    square = jnp.zeros((rows, LANES), F32)
    for cut in tiles:
        h = hidden[:, cut] + jnp.dot(
            normed[final], held[pl.ds(pl.multiple_of(final * block, block), block), cut],
            preferred_element_type=F32,
        )
        hidden[:, cut] = h
        for j in range(0, tile, LANES):
            piece = h[:, j : j + LANES]
            square = square + piece * piece
        moved = jnp.dot(place[...], h.astype(BF16), preferred_element_type=F32).astype(BF16)
        send[:, :, cut] = moved.reshape(n, slot_rows, tile)

    def row_copy(peer):
        return remote(send.at[peer], hid_ref.at[me], a2a_send, a2a_recv, {"fsdp": peer})

    def same_line():
        row_copy(p.sibling).start()

        @pl.loop(1, L)
        def _(k):
            to = lax.rem(p.row + k, L)
            row_copy(p.at(to, p.col, 0)).start()
            row_copy(p.at(to, p.col, 1)).start()

    def other_line(m):
        to = lax.rem(p.row + L // 2 + m, L)
        row_copy(p.at(to, 1 - p.col, 0)).start()
        row_copy(p.at(to, 1 - p.col, 1)).start()

    other_line(0)
    same_line()
    stay = pltpu.make_async_copy(send.at[me], hid_ref.at[me], load_sems.at[2])
    stay.start()

    rinv = lax.rsqrt(jnp.sum(square, -1, keepdims=True) / width + NORM_EPS)
    headb = head[...].astype(BF16)
    heads = jnp.zeros((rows, LANES), F32)
    for j, cut in enumerate(tiles):
        hb = (hidden[:, cut] * rinv).astype(BF16)
        hnorm[:, cut] = hb
        heads = heads + lax.dot_general(
            hb, headb[:, j * tile : (j + 1) * tile], (((1,), (1,)), ((), ())), preferred_element_type=F32
        )
    await_bytes(stats.at[pl.ds(0, n - 1)], stat_recv)
    sums = jnp.sum(stats[...], 0)
    mean_adv = sums[0:1, 0:1] / total_rows
    var_adv = sums[0:1, 1:2] / total_rows - mean_adv * mean_adv
    advant = ((cols[0, :, 0:1] - mean_adv) * lax.rsqrt(var_adv + NORM_EPS)).astype(BF16).astype(F32)
    ret = cols[1, :, 0:1].astype(BF16).astype(F32)
    lane = lax.broadcasted_iota(jnp.int32, (1, LANES), 1)
    one = lax.rem(lane, 16)
    first = lane < 16
    is_act = (one < nact) & (lane < 32)
    is_value = (one == nact) & (lane < 32)
    inv = jnp.where(is_act, jnp.exp(-lstd[0:1, :]), 0.0)
    noise = cols[3]
    u = (cols[2] - heads) * inv
    logr = jnp.sum(jnp.where(first, -noise * u - 0.5 * u * u, 0.0), -1, keepdims=True)
    ratio = jnp.exp(logr)
    scale = 1.0 / jnp.sqrt(jnp.full((1, 1), total_rows, F32))
    clipped = jnp.clip(ratio, 1.0 - CLIP_EPS, 1.0 + CLIP_EPS)
    active = ratio * advant <= clipped * advant
    glogr = jnp.where(active, -scale * advant, 0.0) * ratio
    ghead = jnp.where(is_value, scale * (heads - ret), glogr * (inv * (noise + u)))
    std_part = jnp.sum(glogr * (noise * u + u * u), 0, keepdims=True)
    along = jnp.sum(jnp.where(first, ghead * heads, 0.0), -1, keepdims=True) / width
    pull = rinv * rinv * along

    def two_parts(value):
        high = value.astype(BF16)
        return jnp.where(first, high.astype(F32), value - high.astype(F32)).astype(BF16)

    gscaled = two_parts(ghead * rinv)
    for j, cut in enumerate(tiles):
        g = jnp.dot(gscaled, headb[:, j * tile : (j + 1) * tile], preferred_element_type=F32)
        ghid[:, cut] = (g - hidden[:, cut] * pull).astype(BF16)

    def product(owner, cut):
        index = owner if whole_blocks else owner * shard // block
        value = lax.dot_general(
            normed[index], ghid[:, cut], (((0,), (0,)), ((), ())), preferred_element_type=F32
        )
        if whole_blocks:
            return value
        prod[...] = value
        return prod[pl.ds(pl.multiple_of(lax.rem(owner * shard, block), shard), shard)]

    def target(k):
        up = k < L - 1 - p.row
        return jnp.where(up, L - 1 - k, jnp.where(k < L - 1, k - (L - 1 - p.row), p.row))

    def sib_copy(slot, j):
        return remote(
            sib_out.at[slot, :, tiles[j]], sib_in.at[slot, :, tiles[j]], rs_sib_send, rs_sib_recv.at[slot, j], sibling
        )

    def y_copy(k, j):
        return remote(
            y_out.at[k, :, tiles[j]], y_in.at[k, :, tiles[j]], y_send, y_recv.at[k, j],
            {"fsdp": p.at(p.row, 1 - p.col, p.core)},
        )

    def for_sibling(k, cross):
        slot = 2 * k + cross
        owner = p.at(target(k), (1 - p.col) if cross else p.col, 1 - p.core)
        for j, cut in enumerate(tiles):
            sib_out[slot, :, cut] = product(owner, cut).astype(BF16)
            sib_copy(slot, j).start()

    def for_me(k, cross):
        owner = p.at(target(k), (1 - p.col) if cross else p.col, p.core)
        for cut in tiles:
            own[:, cut] = product(owner, cut)

    def send_y(k):
        for_sibling(k, 1)
        for_me(k, 1)
        for j, cut in enumerate(tiles):
            sib_copy(2 * k + 1, j).wait_recv()
            y_out[k, :, cut] = (own[:, cut] + sib_in[2 * k + 1, :, cut].astype(F32)).astype(BF16)
            y_copy(k, j).start()

    def chip_sum(k, j):
        cut = tiles[j]
        sib_copy(2 * k, j).wait_recv()
        y_copy(k, j).wait_recv()
        return own[:, cut] + sib_in[2 * k, :, cut].astype(F32) + y_in[k, :, cut].astype(F32)

    def z_copy(to, slot, t, j, row):
        return remote(
            z_out.at[t, :, tiles[j]], z_in.at[slot, :, tiles[j]], z_send, z_recv.at[slot, j],
            {"fsdp": p.at(row, p.col, p.core)},
        )

    def z_arrival(slot, j):
        return remote(
            z_out.at[0, :, tiles[j]], z_in.at[slot, :, tiles[j]], z_send, z_recv.at[slot, j],
            {"fsdp": p.sibling},
        )

    send_y(0)

    gparts = two_parts(ghead)
    row = lax.broadcasted_iota(jnp.int32, (16, LANES), 0)
    for j, cut in enumerate(tiles):
        part_sum = lax.dot_general(gparts, hnorm[:, cut], (((0,), (0,)), ((), ())), preferred_element_type=F32)
        both = part_sum[0:16] + part_sum[16:32]
        for i in range(tile // LANES):
            head_blk[j * (tile // LANES) + i] = jnp.where(
                row == nact + 1, std_part, both[:, i * LANES : (i + 1) * LANES]
            )
    nb = head_all.shape[0]
    is_reducer = me < nb

    def when_reducer(go):
        if nb == n:
            go()
        else:
            pl.when(is_reducer)(go)

    def keep_block():
        head_in[me] = head_blk[me]

    when_reducer(keep_block)
    spread(nb, lambda peer: head_blk.at[peer], head_in, head_sems.at[0], head_sems.at[1])

    def reduce_heads():
        def go():
            await_bytes(head_in.at[pl.ds(0, n - 1)], head_sems.at[1])
            head_sum[...] = jnp.sum(head_in[...], 0)
            head_all[me] = head_sum[...]
            spread(n, lambda peer: head_sum, head_all, head_sems.at[2], head_sems.at[3])

        when_reducer(go)

    def stage(k, _):
        other_line(k + 1)
        send_y(k + 1)
        for_sibling(k, 0)
        for_me(k, 0)
        t = target(k)
        up = k < L - 1 - p.row
        has_in = jnp.where(up, p.row > 0, p.row < L - 1)
        to = jnp.where(up, p.row + 1, p.row - 1)
        slot = jnp.where((t == to) & jnp.logical_not(up), L, t)
        for j, cut in enumerate(tiles):
            total = chip_sum(k, j)
            own[:, cut] = total

            @pl.when(has_in)
            def _():
                z_arrival(t, j).wait_recv()
                own[:, cut] += z_in[t, :, cut].astype(F32)

            z_out[t, :, cut] = own[:, cut].astype(BF16)
            z_copy(to, slot, t, j, to).start()

        @pl.when(k == 1)
        def _():
            reduce_heads()

        return 0

    lax.fori_loop(0, L - 1, stage, 0)
    for_sibling(L - 1, 0)
    for_me(L - 1, 0)
    for j, cut in enumerate(tiles):
        grad_ref[:, cut] = chip_sum(L - 1, j)

        @pl.when(p.row > 0)
        def _():
            z_arrival(p.row, j).wait_recv()
            grad_ref[:, cut] += z_in[p.row, :, cut].astype(F32)

        @pl.when(p.row < L - 1)
        def _():
            z_arrival(L, j).wait_recv()
            grad_ref[:, cut] += z_in[L, :, cut].astype(F32)

    if nb == n:
        await_bytes(head_all.at[pl.ds(0, nb - 1)], head_sems.at[3])
    else:
        @pl.when(is_reducer)
        def _():
            await_bytes(head_all.at[pl.ds(0, nb - 1)], head_sems.at[3])

        @pl.when(jnp.logical_not(is_reducer))
        def _():
            await_bytes(head_all.at[pl.ds(0, nb)], head_sems.at[3])

    for j in range(nb):
        headg_ref[:, j * LANES : (j + 1) * LANES] = head_all[j, 0 : nact + 1, :]
    stdg_ref[...] = head_all[0, nact + 1 : nact + 2, 0:nact]
    await_bytes(hid_ref.at[pl.ds(0, n - 1)], a2a_recv)
    stay.wait()
    await_bytes(send.at[pl.ds(0, n - 1)], a2a_send)
    await_bytes(held.at[pl.ds(0, last * shard), pl.ds(0, width - xw)], ring_send)
    await_bytes(held.at[pl.ds(0, last * shard), pl.ds(0, xw)], x_send)
    await_bytes(held.at[pl.ds(0, p.ring * shard)], sib_send)
    await_bytes(stats.at[pl.ds(0, n - 1)], stat_send)
    if nb == n:
        await_bytes(head_blk.at[pl.ds(0, nb - 1)], head_sems.at[0])
        await_bytes(head_in.at[pl.ds(0, n - 1)], head_sems.at[2])
    else:
        @pl.when(is_reducer)
        def _():
            await_bytes(head_blk.at[pl.ds(0, nb - 1)], head_sems.at[0])
            await_bytes(head_in.at[pl.ds(0, n - 1)], head_sems.at[2])

        @pl.when(jnp.logical_not(is_reducer))
        def _():
            await_bytes(head_blk.at[pl.ds(0, nb)], head_sems.at[0])

    await_bytes(sib_out, rs_sib_send)
    await_bytes(y_out, y_send)
    await_bytes(z_out.at[pl.ds(0, L - 1)], z_send)


def local(
    obs_feat, reward, value_old, done, minibatch_perm, old_mean, noise, gain_in, out_weight, head_weight, log_std
):
    rows, width = obs_feat.shape
    n = lax.axis_size("fsdp")
    steps = reward.shape[1]
    n_env = reward.shape[0]
    nact = log_std.shape[0]
    shard = out_weight.shape[0]
    block = max(shard, LANES)
    per = rows // n
    slot_rows = -(-per // 8) * 8
    L = n // 4
    ring = n // 2
    nb = min(n, width // LANES)
    vmem = pl.BlockSpec(memory_space=pltpu.VMEM)
    hbm = pl.BlockSpec(memory_space=pl.ANY)
    sem = pltpu.SemaphoreType.DMA
    V = pltpu.VMEM
    hid, grad, headg, stdg = pl.pallas_call(
        functools.partial(kernel, n, steps),
        name="step",
        out_shape=(
            jax.ShapeDtypeStruct((n, slot_rows, width), BF16),
            jax.ShapeDtypeStruct((shard, width), F32),
            jax.ShapeDtypeStruct((nact + 1, width), F32),
            jax.ShapeDtypeStruct((1, nact), F32),
        ),
        in_specs=[hbm, hbm] + [vmem] * 9,
        out_specs=(hbm, vmem, vmem, vmem),
        scratch_shapes=[
            V((rows, width), BF16),
            V((width, width), BF16),
            V((width // block, rows, block), BF16),
            V((rows, width), F32),
            V((rows, width), BF16),
            V((rows, width), BF16),
            V((n * slot_rows, rows), BF16),
            V((n, slot_rows, width), BF16),
            V((LANES, rows), F32),
            V((4, rows, LANES), F32),
            V((4, n_env, LANES), F32),
            V((LANES, width), F32),
            V((8, LANES), F32),
            V((n, 8, LANES), F32),
            V((8, LANES), F32),
            V((nb, 16, LANES), F32),
            V((n, 16, LANES), F32),
            V((16, LANES), F32),
            V((nb, 16, LANES), F32),
            V((2 * L, shard, width), BF16),
            V((2 * L, shard, width), BF16),
            V((L, shard, width), BF16),
            V((L, shard, width), BF16),
            V((L, shard, width), BF16),
            V((L + 1, shard, width), BF16),
            V((shard, width), F32),
            V((block, width // 4), F32),
            sem((3,)),
            sem(()),
            sem((ring, 4)),
            sem(()),
            sem((ring, 2)),
            sem((ring, 4)),
            sem((ring, 2)),
            sem(()),
            sem(()),
            sem(()),
            sem(()),
            sem(()),
            sem((4,)),
            sem(()),
            sem((2 * L, 4)),
            sem(()),
            sem((L, 4)),
            sem(()),
            sem((L + 1, 4)),
        ],
        compiler_params=pltpu.CompilerParams(
            collective_id=0, has_side_effects=True, vmem_limit_bytes=60 << 20
        ),
        cost_estimate=pl.CostEstimate(
            flops=4 * rows * width * width, bytes_accessed=16 * rows * width, transcendentals=0
        ),
    )(
        obs_feat, out_weight, gain_in[None, :], reward, value_old, done, minibatch_perm[None, :],
        old_mean.T, noise.T, head_weight.T, log_std[None, :],
    )
    hid = hid[:, :per].reshape(rows, width)
    return (hid, grad, headg.T, stdg[0])


def solution(mesh):
    both = P(("groups", "fsdp"), None)
    return jax.shard_map(
        local,
        mesh=mesh,
        in_specs=(
            both, both, both, both, P(("groups", "fsdp")), both, both, P(), P("fsdp", None), P(), P(),
        ),
        out_specs=(both, both, P("groups", None), P("groups")),
        check_vma=False,
    )
```

time: 167 us -> 130 us (0.78)
  the two profiles are of different devices: /device:TPU:0 before, /device:TPU:16 now
where the time goes in v1:
time: 130 us; the launch traced here: 129 us
  Pallas kernels  123 us (95%)
  local copies, waits for them, and re-layouts  6.23 us (5%)
    pallas_call x1, Pallas kernels, local(): pl.pallas_call(functools.partial(kernel, n, steps), name='step', out_shap...  123 us
    unnamed x10, local copies, waits for them, and re-layouts  4.99 us

profile of v1, /device:TPU:16, one launch (start us, length us, event | category | flops | bytes accessed | tf_op | source)
XLA Modules:
  0.0 129.4 jit_solution(13657371709845595478)
XLA Ops:
  0.6 1.2 broadcast_in_dim.10.perm_ref
  1.9 122.5 %step.1 = (bf16[16,24,2048]{2,1,0:T(8,128)(2,1)}, f32[128,2048]{1,0:T(8,128)}, f32[13,2048]{1,0:T(8,128)}, f32[1,12]{1,0:T(1,128)}) custom-call(bf16[384,2048]{1,0:T(8,128)(2,1)} %x_hbm.1, bf16[128,2048]{1,0:T(8,128)(2,1)} %w_hbm.1, f32[1,2048]{1,0:T(1,128)} %bitcast.13, f32[16,24]{1,0:T(8,128)} %reward_ref.1, f32[16,25]{1,0:T(8,128)} %value_ref.1, ...), custom_call_target="tpu_custom_call" | custom-call | flops 6442450944 | bytes 12582912 | tf_op jit(solution)/shard_map/step/pallas_call | solution.py:583
  124.4 0.0 copy-start
  124.4 2.8 %copy.19 = bf16[384,2048]{1,0:T(8,128)(2,1)} copy(bf16[384,2048]{1,0:T(8,128)(2,1)} %bitcast.8) | data formatting | bytes 3145728
  127.2 0.0 copy-done
  127.2 0.0 copy-start.1
  127.2 0.0 copy-start.2
  127.2 1.0 copy.20
  128.2 0.0 copy-done.1
  128.2 0.7 copy.21
  128.9 0.0 copy-done.2
  128.9 0.5 copy.22
Async XLA Ops:
  124.4 2.8 %copy-start = (f32[128,2048]{1,0:T(8,128)S(1)}, f32[128,2048]{1,0:T(8,128)}, u32[]{:S(2)}) copy-start(f32[128,2048]{1,0:T(8,128)} %get-tuple-element.17) | copy-start | bytes 3145732
  127.2 1.0 copy-start.1
  127.2 1.7 %copy-start.2 = (f32[1,12]{1,0:T(1,128)S(1)}, f32[1,12]{1,0:T(1,128)}, u32[]{:S(2)}) copy-start(f32[1,12]{1,0:T(1,128)} %get-tuple-element.11) | copy-start | bytes 148

commit v2 on v1

--- a/solution.py
+++ b/solution.py
@@ -218,7 +218,7 @@
                 )
 
     def placement():
-        perm = perm_ref[...]
+        perm = perm_ref[...].reshape(1, rows)
         to = lax.div(perm, rows)
         slot = to * slot_rows + lax.rem(perm, per)
         place[...] = jnp.where(
@@ -390,9 +390,17 @@
         prod[...] = value
         return prod[pl.ds(pl.multiple_of(lax.rem(owner * shard, block), shard), shard)]
 
+    def goes_up(k):
+        up_first = 2 * p.row < L
+        return jnp.where(up_first, k < L - 1 - p.row, (k >= p.row) & (k < L - 1))
+
     def target(k):
-        up = k < L - 1 - p.row
-        return jnp.where(up, L - 1 - k, jnp.where(k < L - 1, k - (L - 1 - p.row), p.row))
+        ups, downs = L - 1 - p.row, p.row
+        up_first = 2 * p.row < L
+        up_at = jnp.where(up_first, k, k - downs)
+        down_at = jnp.where(up_first, k - ups, k)
+        up = goes_up(k)
+        return jnp.where(up, L - 1 - up_at, jnp.where(k < L - 1, down_at, p.row))
 
     def sib_copy(slot, j):
         return remote(
@@ -415,26 +423,26 @@
     def for_me(k, cross):
         owner = p.at(target(k), (1 - p.col) if cross else p.col, p.core)
         for cut in tiles:
-            own[:, cut] = product(owner, cut)
+            own[k, :, cut] = product(owner, cut)
 
     def send_y(k):
         for_sibling(k, 1)
         for_me(k, 1)
         for j, cut in enumerate(tiles):
             sib_copy(2 * k + 1, j).wait_recv()
-            y_out[k, :, cut] = (own[:, cut] + sib_in[2 * k + 1, :, cut].astype(F32)).astype(BF16)
+            y_out[k, :, cut] = (own[k, :, cut] + sib_in[2 * k + 1, :, cut].astype(F32)).astype(BF16)
             y_copy(k, j).start()
 
     def chip_sum(k, j):
         cut = tiles[j]
         sib_copy(2 * k, j).wait_recv()
         y_copy(k, j).wait_recv()
-        return own[:, cut] + sib_in[2 * k, :, cut].astype(F32) + y_in[k, :, cut].astype(F32)
-
-    def z_copy(to, slot, t, j, row):
+        return own[k, :, cut] + sib_in[2 * k, :, cut].astype(F32) + y_in[k, :, cut].astype(F32)
+
+    def z_copy(to, slot, k, j):
         return remote(
-            z_out.at[t, :, tiles[j]], z_in.at[slot, :, tiles[j]], z_send, z_recv.at[slot, j],
-            {"fsdp": p.at(row, p.col, p.core)},
+            z_out.at[k, :, tiles[j]], z_in.at[slot, :, tiles[j]], z_send, z_recv.at[slot, j],
+            {"fsdp": p.at(to, p.col, p.core)},
         )
 
     def z_arrival(slot, j):
@@ -478,27 +486,37 @@
 
         when_reducer(go)
 
-    def stage(k, _):
-        other_line(k + 1)
-        send_y(k + 1)
+    def first_stage(k, _):
+        other_line(k)
+        send_y(k)
+        return 0
+
+    lax.fori_loop(1, L, first_stage, 0)
+
+    def second_stage(k, _):
         for_sibling(k, 0)
         for_me(k, 0)
+        return 0
+
+    lax.fori_loop(0, L, second_stage, 0)
+
+    def third_stage(k, _):
         t = target(k)
-        up = k < L - 1 - p.row
+        up = goes_up(k)
         has_in = jnp.where(up, p.row > 0, p.row < L - 1)
         to = jnp.where(up, p.row + 1, p.row - 1)
         slot = jnp.where((t == to) & jnp.logical_not(up), L, t)
         for j, cut in enumerate(tiles):
             total = chip_sum(k, j)
-            own[:, cut] = total
+            own[k, :, cut] = total
 
             @pl.when(has_in)
             def _():
                 z_arrival(t, j).wait_recv()
-                own[:, cut] += z_in[t, :, cut].astype(F32)
-
-            z_out[t, :, cut] = own[:, cut].astype(BF16)
-            z_copy(to, slot, t, j, to).start()
+                own[k, :, cut] += z_in[t, :, cut].astype(F32)
+
+            z_out[k, :, cut] = own[k, :, cut].astype(BF16)
+            z_copy(to, slot, k, j).start()
 
         @pl.when(k == 1)
         def _():
@@ -506,9 +524,7 @@
 
         return 0
 
-    lax.fori_loop(0, L - 1, stage, 0)
-    for_sibling(L - 1, 0)
-    for_me(L - 1, 0)
+    lax.fori_loop(0, L - 1, third_stage, 0)
     for j, cut in enumerate(tiles):
         grad_ref[:, cut] = chip_sum(L - 1, j)
 
@@ -584,13 +600,13 @@
         functools.partial(kernel, n, steps),
         name="step",
         out_shape=(
-            jax.ShapeDtypeStruct((n, slot_rows, width), BF16),
-            jax.ShapeDtypeStruct((shard, width), F32),
-            jax.ShapeDtypeStruct((nact + 1, width), F32),
-            jax.ShapeDtypeStruct((1, nact), F32),
+            V((n, slot_rows, width), BF16),
+            V((shard, width), F32),
+            V((nact + 1, width), F32),
+            V((1, nact), F32),
         ),
         in_specs=[hbm, hbm] + [vmem] * 9,
-        out_specs=(hbm, vmem, vmem, vmem),
+        out_specs=(vmem, vmem, vmem, vmem),
         scratch_shapes=[
             V((rows, width), BF16),
             V((width, width), BF16),
@@ -617,7 +633,7 @@
             V((L, shard, width), BF16),
             V((L, shard, width), BF16),
             V((L + 1, shard, width), BF16),
-            V((shard, width), F32),
+            V((L, shard, width), F32),
             V((block, width // 4), F32),
             sem((3,)),
             sem(()),
@@ -640,13 +656,13 @@
             sem((L + 1, 4)),
         ],
         compiler_params=pltpu.CompilerParams(
-            collective_id=0, has_side_effects=True, vmem_limit_bytes=60 << 20
+            collective_id=0, has_side_effects=True, vmem_limit_bytes=54 << 20
         ),
         cost_estimate=pl.CostEstimate(
             flops=4 * rows * width * width, bytes_accessed=16 * rows * width, transcendentals=0
         ),
     )(
-        obs_feat, out_weight, gain_in[None, :], reward, value_old, done, minibatch_perm[None, :],
+        obs_feat, out_weight, gain_in[None, :], reward, value_old, done, minibatch_perm,
         old_mean.T, noise.T, head_weight.T, log_std[None, :],
     )
     hid = hid[:, :per].reshape(rows, width)

time: 130 us -> 119 us (0.915)
  the two profiles are of different devices: /device:TPU:16 before, /device:TPU:0 now
where the time goes in v2:
time: 119 us; the launch traced here: 118 us
  Pallas kernels  114 us (96%)
  local copies, waits for them, and re-layouts  3.28 us (3%)
    pallas_call x1, Pallas kernels, local(): pl.pallas_call(functools.partial(kernel, n, steps), name='step', out_shap...  114 us
    unnamed x4, local copies, waits for them, and re-layouts  3.28 us

profile of v2, /device:TPU:0, one launch (start us, length us, event | category | flops | bytes accessed | tf_op | source)
XLA Modules:
  0.0 118.4 jit_solution(7430348617519877319)
XLA Ops:
  0.6 114.5 %step.1 = (bf16[16,24,2048]{2,1,0:T(8,128)(2,1)S(1)}, f32[128,2048]{1,0:T(8,128)S(1)}, f32[13,2048]{1,0:T(8,128)S(1)}, f32[1,12]{1,0:T(1,128)S(1)}) custom-call(bf16[384,2048]{1,0:T(8,128)(2,1)} %x_hbm.1, bf16[128,2048]{1,0:T(8,128)(2,1)} %w_hbm.1, f32[1,2048]{1,0:T(1,128)} %bitcast.14, f32[16,24]{1,0:T(8,128)} %reward_ref.1, f32[16,25]{1,0:T(8,128)} %value_ref.1, ...), custom_call_target="tpu_custom_call" | custom-call | flops 6442450944 | bytes 12582912 | tf_op jit(solution)/shard_map/step/pallas_call | solution.py:599
  115.1 1.1 copy.19
  116.3 0.5 copy.22
  116.8 0.7 copy.21
  117.4 1.0 copy.20

commit v3 on v2

--- a/solution.py
+++ b/solution.py
@@ -285,55 +285,83 @@
         return 0
 
     lax.fori_loop(1, p.ring, hop, 0)
-    for i in range(2):
-        x_arrival(mine(last), last, i).wait_recv()
-        sibx_copy(mine(last), last, i).start()
-    for s in (last - 1, last):
-        other = theirs(s)
-        if s == last:
-            add_shard(mine(last))
-        for i in range(4):
-            sibr_copy(other, s, i).wait_recv()
+    def term(index, cut):
+        rows_at = pl.ds(pl.multiple_of(index * block, block), block)
+        return jnp.dot(normed[index], held[rows_at, lanes(*cut)], preferred_element_type=F32)
+
+    def last_x():
         for i in range(2):
-            sibx_copy(other, s, i).wait_recv()
-        if s < last:
-            add_shard(other)
-    if not whole_blocks:
-        lax.fori_loop(0, width // block - 1, lambda b, _: (add(b), 0)[1], 0)
-    final = theirs(last) if whole_blocks else width // block - 1
-
-    square = jnp.zeros((rows, LANES), F32)
-    for cut in tiles:
-        h = hidden[:, cut] + jnp.dot(
-            normed[final], held[pl.ds(pl.multiple_of(final * block, block), block), cut],
-            preferred_element_type=F32,
-        )
-        hidden[:, cut] = h
-        for j in range(0, tile, LANES):
+            x_arrival(mine(last), last, i).wait_recv()
+            sibx_copy(mine(last), last, i).start()
+
+    def await_sibling(s, ring_part, x_part):
+        if ring_part:
+            for i in range(4):
+                sibr_copy(theirs(s), s, i).wait_recv()
+        if x_part:
+            for i in range(2):
+                sibx_copy(theirs(s), s, i).wait_recv()
+
+    await_sibling(last - 1, True, True)
+    if whole_blocks:
+        pair = (mine(last), theirs(last))
+        add(theirs(last - 1))
+    else:
+        last_x()
+        await_sibling(last, True, True)
+        lax.fori_loop(0, width // block - 2, lambda b, _: (add(b), 0)[1], 0)
+        pair = (width // block - 2, width // block - 1)
+
+    def finish(cut, square):
+        h = hidden[:, lanes(*cut)] + term(pair[0], cut) + term(pair[1], cut)
+        hidden[:, lanes(*cut)] = h
+        for j in range(0, cut[1], LANES):
             piece = h[:, j : j + LANES]
             square = square + piece * piece
         moved = jnp.dot(place[...], h.astype(BF16), preferred_element_type=F32).astype(BF16)
-        send[:, :, cut] = moved.reshape(n, slot_rows, tile)
-
-    def row_copy(peer):
-        return remote(send.at[peer], hid_ref.at[me], a2a_send, a2a_recv, {"fsdp": peer})
-
-    def same_line():
-        row_copy(p.sibling).start()
+        send[:, :, lanes(*cut)] = moved.reshape(n, slot_rows, cut[1])
+        return square
+
+    ring_part = (p.group * xw, width - xw)
+    x_part = ((1 - p.group) * (width - xw), xw)
+
+    def row_copy(peer, cut):
+        return remote(
+            send.at[peer, :, lanes(*cut)], hid_ref.at[me, :, lanes(*cut)], a2a_send, a2a_recv, {"fsdp": peer}
+        )
+
+    def same_line(cut):
+        row_copy(p.sibling, cut).start()
 
         @pl.loop(1, L)
         def _(k):
             to = lax.rem(p.row + k, L)
-            row_copy(p.at(to, p.col, 0)).start()
-            row_copy(p.at(to, p.col, 1)).start()
-
-    def other_line(m):
+            row_copy(p.at(to, p.col, 0), cut).start()
+            row_copy(p.at(to, p.col, 1), cut).start()
+
+    def other_line(m, cut):
         to = lax.rem(p.row + L // 2 + m, L)
-        row_copy(p.at(to, 1 - p.col, 0)).start()
-        row_copy(p.at(to, 1 - p.col, 1)).start()
-
-    other_line(0)
-    same_line()
+        row_copy(p.at(to, 1 - p.col, 0), cut).start()
+        row_copy(p.at(to, 1 - p.col, 1), cut).start()
+
+    square = jnp.zeros((rows, LANES), F32)
+    for i, cut in enumerate(ring_cuts):
+        if whole_blocks:
+            sibr_copy(theirs(last), last, i).wait_recv()
+        square = finish(cut, square)
+
+    @pl.loop(0, L - 1)
+    def _(m):
+        other_line(m, ring_part)
+
+    same_line(ring_part)
+    if whole_blocks:
+        last_x()
+    for i, cut in enumerate(x_cuts):
+        if whole_blocks:
+            sibx_copy(theirs(last), last, i).wait_recv()
+        square = finish(cut, square)
+    same_line(x_part)
     stay = pltpu.make_async_copy(send.at[me], hid_ref.at[me], load_sems.at[2])
     stay.start()
 
@@ -452,6 +480,7 @@
         )
 
     send_y(0)
+    other_line(0, x_part)
 
     gparts = two_parts(ghead)
     row = lax.broadcasted_iota(jnp.int32, (16, LANES), 0)
@@ -487,7 +516,11 @@
         when_reducer(go)
 
     def first_stage(k, _):
-        other_line(k)
+        @pl.when(k == 1)
+        def _():
+            other_line(L - 1, ring_part)
+
+        other_line(k, x_part)
         send_y(k)
         return 0
 
@@ -575,6 +608,17 @@
     await_bytes(sib_out, rs_sib_send)
     await_bytes(y_out, y_send)
     await_bytes(z_out.at[pl.ds(0, L - 1)], z_send)
+
+
+def store_kernel(a, b, c, d, a_out, b_out, c_out, d_out, sems):
+    copies = [
+        pltpu.make_async_copy(src, dst, sems.at[i])
+        for i, (src, dst) in enumerate(((a, a_out), (b, b_out), (c, c_out), (d, d_out)))
+    ]
+    for copy in copies:
+        copy.start()
+    for copy in copies:
+        copy.wait()
 
 
 def local(
@@ -665,6 +709,16 @@
         obs_feat, out_weight, gain_in[None, :], reward, value_old, done, minibatch_perm,
         old_mean.T, noise.T, head_weight.T, log_std[None, :],
     )
+    results = (hid, grad, headg, stdg)
+    hid, grad, headg, stdg = pl.pallas_call(
+        store_kernel,
+        name="store",
+        out_shape=tuple(jax.ShapeDtypeStruct(r.shape, r.dtype) for r in results),
+        in_specs=[hbm] * 4,
+        out_specs=(hbm,) * 4,
+        scratch_shapes=[sem((4,))],
+        compiler_params=pltpu.CompilerParams(vmem_limit_bytes=1 << 20),
+    )(*results)
     hid = hid[:, :per].reshape(rows, width)
     return (hid, grad, headg.T, stdg[0])
 

time: 119 us -> 113 us (0.950)
  local copies, waits for them, and re-layouts: 3.28 us -> 0 us
  Pallas kernels: 114 us -> 112 us
    pallas_call x1, Pallas kernels: 114 us -> 110 us  [local(): pl.pallas_call(functools.partial(kernel, n, steps), name='step', out_shap...]
    unnamed x4 -> x0, local copies, waits for them, and re-layouts: 3.28 us -> none
    pallas_call x0 -> x1, Pallas kernels: none -> 1.56 us  [local(): pl.pallas_call(store_kernel, name='store', out_shape=tuple((jax.ShapeDtyp...]
where the time goes in v3:
time: 113 us; the launch traced here: 112 us
  Pallas kernels  112 us (99%)
    pallas_call x1, Pallas kernels, local(): pl.pallas_call(functools.partial(kernel, n, steps), name='step', out_shap...  110 us

profile of v3, /device:TPU:0, one launch (start us, length us, event | category | flops | bytes accessed | tf_op | source)
XLA Modules:
  0.0 112.4 jit_solution(2396680464627296953)
XLA Ops:
  0.6 110.2 %step.1 = (bf16[16,24,2048]{2,1,0:T(8,128)(2,1)S(1)}, f32[128,2048]{1,0:T(8,128)S(1)}, f32[13,2048]{1,0:T(8,128)S(1)}, f32[1,12]{1,0:T(1,128)S(1)}) custom-call(bf16[384,2048]{1,0:T(8,128)(2,1)} %x_hbm.1, bf16[128,2048]{1,0:T(8,128)(2,1)} %w_hbm.1, f32[1,2048]{1,0:T(1,128)} %bitcast.13, f32[16,24]{1,0:T(8,128)} %reward_ref.1, f32[16,25]{1,0:T(8,128)} %value_ref.1, ...), custom_call_target="tpu_custom_call" | custom-call | flops 6442450944 | bytes 12582912 | tf_op jit(solution)/shard_map/step/pallas_call | solution.py:643
  110.8 1.6 %store.1 = (bf16[16,24,2048]{2,1,0:T(8,128)(2,1)}, f32[128,2048]{1,0:T(8,128)}, f32[13,2048]{1,0:T(8,128)}, f32[1,12]{1,0:T(1,128)}) custom-call(bf16[16,24,2048]{2,1,0:T(8,128)(2,1)S(1)} %get-tuple-element.12.a, f32[128,2048]{1,0:T(8,128)S(1)} %get-tuple-element.13.b, f32[13,2048]{1,0:T(8,128)S(1)} %get-tuple-element.14.c, f32[1,12]{1,0:T(1,128)S(1)} %get-tuple-element.15.d), custom_call_target="tpu_custom_call" | custom-call | tf_op jit(solution)/shard_map/store/pallas_call | solution.py:713

commit v4 on v3

--- a/solution.py
+++ b/solution.py
@@ -17,34 +17,29 @@
 BF16 = jnp.bfloat16
 
 
-def chip_at(pos, ring):
-    half = ring // 2
-    col = pos // half
-    row = col * (ring - 1 - pos) + (1 - col) * pos
-    return 2 * row + col
-
-
 class Place:
     def __init__(self, n):
-        self.n = n
         self.me = lax.axis_index("fsdp")
         self.group = lax.axis_index("groups")
-        self.ring = n // 2
         self.rows = n // 4
         self.core = lax.rem(self.me, 2)
         chip = self.me // 2
         self.col = lax.rem(chip, 2)
         self.row = chip // 2
-        self.pos = self.col * (self.ring - 1 - self.row) + (1 - self.col) * self.row
-        self.step = 1 - 2 * self.core
-        self.sibling = self.me + self.step
-
-    def on_ring(self, ahead, core):
-        pos = lax.rem(self.pos + ahead + self.ring, self.ring)
-        return 2 * chip_at(pos, self.ring) + core
+        self.sibling = self.me + 1 - 2 * self.core
+        self.across = self.at(self.row, 1 - self.col, self.core)
+        self.at_end = (self.row == 0) | (self.row == self.rows - 1)
 
     def at(self, row, col, core):
         return (row * 2 + col) * 2 + core
+
+    def nth_row(self, q):
+        below, above = self.row, self.rows - 1 - self.row
+        near = jnp.minimum(below, above)
+        toward = jnp.where(below < above, 1, -1)
+        inner = self.row + toward * jnp.where(lax.rem(q, 2) == 1, -((q + 1) // 2), q // 2)
+        outer = self.row + toward * (q - near)
+        return jnp.where(q <= 2 * near, inner, outer)
 
 
 def remote(src, dst, send, recv, device):
@@ -57,9 +52,13 @@
     pltpu.make_async_copy(part, part, sem).wait()
 
 
-def halves(start, size):
-    first = (size // LANES + 1) // 2 * LANES
-    return [(start, first), (start + first, size - first)]
+def cuts_of(start, size, count):
+    blocks, cuts = size // LANES, []
+    for i in range(count):
+        take = -(-blocks // (count - i))
+        cuts.append((start, take * LANES))
+        start, blocks = start + take * LANES, blocks - take
+    return cuts
 
 
 def lanes(start, size):
@@ -72,13 +71,15 @@
     hid_ref, grad_ref, headg_ref, stdg_ref,
     xv, held, normed, hidden, hnorm, ghid, place, send, rows_t, cols, envs, head, lstd,
     stats, stat_own, head_blk, head_in, head_sum, head_all,
-    sib_out, sib_in, y_out, y_in, z_out, z_in, own, prod,
-    load_sems, ring_send, ring_recv, x_send, x_recv, sibr_recv, sibx_recv, sib_send,
+    sib_out, sib_in, y_out, y_in, z_out, z_in, zq_out, zq_in, yq_out, yq_in, own, ownz, normed_t, layer,
+    obs_send, ext_in, ext_out, normed_e,
+    load_sems, z_ag_send, z_ag_recv, y_ag_send, y_ag_recv, x_send, x_recv, sibr_recv, sibx_recv, sib_send,
+    ext_send, ext_recv, fwd_send,
     stat_send, stat_recv, a2a_send, a2a_recv, head_sems,
-    rs_sib_send, rs_sib_recv, y_send, y_recv, z_send, z_recv,
+    rs_sib_send, rs_sib_recv, y_send, y_recv, z_send, z_recv, zq_send, zq_recv, yq_send, yq_recv,
 ):
     p = Place(n)
-    me, last, L = p.me, p.ring - 1, p.rows
+    me, L = p.me, p.rows
     rows, width = xv.shape
     shard = w_hbm.shape[0]
     block = normed.shape[2]
@@ -96,6 +97,7 @@
     load_w = pltpu.make_async_copy(w_hbm, held.at[pl.ds(pl.multiple_of(me * shard, shard), shard)], load_sems.at[1])
     load_w.start()
 
+    ext_in[...] = jnp.zeros_like(ext_in)
     barrier = pltpu.get_barrier_semaphore()
 
     @pl.loop(1, n)
@@ -103,54 +105,84 @@
         pl.semaphore_signal(barrier, inc=1, device_id={"fsdp": lax.rem(me + k, n)}, device_id_type=MESH)
 
     pl.semaphore_signal(barrier, inc=1, device_id={"groups": 1 - p.group}, device_id_type=MESH)
+
+    perm = perm_ref[...].reshape(1, rows)
+    slot_of = lax.div(perm, rows) * slot_rows + lax.rem(perm, per)
+    place[...] = jnp.where(lax.broadcasted_iota(jnp.int32, place.shape, 0) == slot_of, 1.0, 0.0).astype(BF16)
+    load_x.wait()
+
+    @pl.when(p.at_end)
+    def _():
+        for cut in tiles:
+            moved = jnp.dot(place[...], xv[:, cut], preferred_element_type=F32).astype(BF16)
+            obs_send[:, :, cut] = moved.reshape(n, slot_rows, tile)
+
     pl.semaphore_wait(barrier, n)
 
     xw = width // LANES * 5 // 16 * LANES
     rest = width - 2 * xw
-    ring_cuts = halves(p.group * (width - xw), xw) + halves(xw, rest)
-    x_cuts = halves((1 - p.group) * (width - xw), xw)
-    next_chip = {"fsdp": p.on_ring(p.step, p.core)}
+    ring_cuts = cuts_of(p.group * (width - xw), xw, 2) + cuts_of(xw, rest, 2)
+    x_cuts = cuts_of((1 - p.group) * (width - xw), xw, 2)
     sibling = {"fsdp": p.sibling}
     partner = {"groups": 1 - p.group}
-
-    def part(owner, cut):
-        return held.at[pl.ds(pl.multiple_of(owner * shard, shard), shard), lanes(*cut)]
-
-    def ring_copy(owner, s, i):
-        ref = part(owner, ring_cuts[i])
-        return remote(ref, ref, ring_send, ring_recv.at[s, i], next_chip)
-
-    def x_copy(owner, s, i):
-        ref = part(owner, ring_cuts[i])
-        return remote(ref, ref, x_send, x_recv.at[s, i], partner)
-
-    def x_arrival(owner, s, i):
-        ref = part(owner, x_cuts[i])
-        return remote(ref, ref, x_send, x_recv.at[s, i], partner)
-
-    def sibr_copy(owner, s, i):
-        ref = part(owner, ring_cuts[i])
-        return remote(ref, ref, sib_send, sibr_recv.at[s, i], sibling)
-
-    def sibx_copy(owner, s, i):
-        ref = part(owner, x_cuts[i])
-        return remote(ref, ref, sib_send, sibx_recv.at[s, i], sibling)
-
-    def mine(s):
-        return p.on_ring(-p.step * s, p.core)
-
-    def theirs(s):
-        return p.on_ring(p.step * s, 1 - p.core)
+    across = {"fsdp": p.across}
+
+    def owner(row, line, core):
+        return p.at(row, p.col if line == 0 else 1 - p.col, core)
+
+    def part(device, cut):
+        return held.at[pl.ds(pl.multiple_of(device * shard, shard), shard), lanes(*cut)]
+
+    def z_ag(o, i, to):
+        ref = part(owner(o, 0, p.core), ring_cuts[i])
+        return remote(ref, ref, z_ag_send, z_ag_recv.at[o, i], {"fsdp": p.at(to, p.col, p.core)})
+
+    def y_ag(o, line, i):
+        ref = part(owner(o, line, p.core), ring_cuts[i])
+        return remote(ref, ref, y_ag_send, y_ag_recv.at[o, i], across)
+
+    def x_ag(o, line, i, cuts):
+        ref = part(owner(o, line, p.core), cuts[i])
+        return remote(ref, ref, x_send, x_recv.at[2 * o + line, i], partner)
+
+    def sibr(o, line, i, core):
+        ref = part(owner(o, line, core), ring_cuts[i])
+        return remote(ref, ref, sib_send, sibr_recv.at[2 * o + line, i], sibling)
+
+    def sibx(o, line, i, core):
+        ref = part(owner(o, line, core), x_cuts[i])
+        return remote(ref, ref, sib_send, sibx_recv.at[2 * o + line, i], sibling)
+
+    def ext_copies(to):
+        for core in range(2):
+            for kind in range(2):
+                block_of = p.at(to, p.col if kind == 0 else 1 - p.col, core)
+                slot = (jnp.where(p.row > 0, 2, 0) + p.core) * 2 + kind
+                remote(
+                    obs_send.at[block_of], ext_in.at[slot], ext_send, ext_recv,
+                    {"fsdp": p.at(to, p.col, core)},
+                ).start()
 
     load_w.wait()
     for i in range(4):
-        ring_copy(me, 1, i).start()
+        @pl.when(p.row > 0)
+        def _():
+            z_ag(p.row, i, p.row - 1).start()
+
+        @pl.when(p.row < L - 1)
+        def _():
+            z_ag(p.row, i, p.row + 1).start()
+
+        y_ag(p.row, 0, i).start()
     for i in range(4):
-        sibr_copy(me, 0, i).start()
+        sibr(p.row, 0, i, p.core).start()
     for i in range(2):
-        sibx_copy(me, 0, i).start()
-
-    load_x.wait()
+        sibx(p.row, 0, i, p.core).start()
+
+    @pl.when(p.at_end)
+    def _():
+        ext_copies(jnp.where(p.row > 0, p.row - 1, p.row + 1))
+
     square = jnp.zeros((rows, LANES), F32)
     for j in range(0, width, LANES):
         xf = xv[:, j : j + LANES].astype(F32)
@@ -169,9 +201,9 @@
                 preferred_element_type=F32,
             )
 
-    def add_shard(owner):
+    def add_shard(device):
         if whole_blocks:
-            add(owner)
+            add(device)
 
     def spread(count, source_of, dst, send_sem, recv_sem):
         @pl.loop(1, n)
@@ -217,20 +249,14 @@
                     jnp.sum(jnp.where(at_step, line, 0.0), -1, keepdims=True), (steps, LANES)
                 )
 
-    def placement():
-        perm = perm_ref[...].reshape(1, rows)
-        to = lax.div(perm, rows)
-        slot = to * slot_rows + lax.rem(perm, per)
-        place[...] = jnp.where(
-            lax.broadcasted_iota(jnp.int32, place.shape, 0) == slot, 1.0, 0.0
-        ).astype(BF16)
-
     def columns():
         for k, ref in ((0, mean_ref), (1, noise_ref)):
             rows_t[...] = jnp.zeros_like(rows_t)
             rows_t[0:nact] = ref[...].astype(F32)
             rows_t[16 : 16 + nact] = ref[...].astype(F32)
             cols[2 + k] = jnp.transpose(rows_t[...])
+        for j in range(width // block):
+            normed_t[j * block : (j + 1) * block] = jnp.transpose(normed[j].astype(F32)).astype(BF16)
         head[...] = jnp.zeros_like(head)
         hf = head_ref[...].astype(F32)
         head[0 : nact + 1] = hf
@@ -239,76 +265,105 @@
         lstd[0:1, 0:nact] = std_ref[...]
         lstd[0:1, 16 : 16 + nact] = std_ref[...]
 
-    def hop(s, _):
-        owner = mine(s)
+    def z_arrives(o):
+        to = jnp.where(o < p.row, p.row + 1, p.row - 1)
         for i in range(4):
-            ring_copy(owner, s, i).wait_recv()
-
-            @pl.when(s < last)
+            z_ag(o, i, p.row).wait_recv()
+
+            @pl.when((to >= 0) & (to < L))
             def _():
-                ring_copy(owner, s + 1, i).start()
-
+                z_ag(o, i, to).start()
+
+            y_ag(o, 0, i).start()
             if i < 2:
-                x_copy(owner, s, i).start()
-            sibr_copy(owner, s, i).start()
-        before = mine(s - 1)
-
-        @pl.when(s > 1)
-        def _():
-            for i in range(2):
-                x_arrival(before, s - 1, i).wait_recv()
-                sibx_copy(before, s - 1, i).start()
-
-        add_shard(before)
-
-        @pl.when(s == 1)
+                x_ag(o, 0, i, ring_cuts).start()
+            sibr(o, 0, i, p.core).start()
+
+    def y_arrives(o, pieces):
+        for i in pieces:
+            y_ag(o, 1, i).wait_recv()
+            if i < 2:
+                x_ag(o, 1, i, ring_cuts).start()
+            sibr(o, 1, i, p.core).start()
+
+    def x_arrives(o, line):
+        for i in range(2):
+            x_ag(o, line, i, x_cuts).wait_recv()
+            sibx(o, line, i, p.core).start()
+
+    def sib_arrives(o, line):
+        for i in range(4):
+            sibr(o, line, i, 1 - p.core).wait_recv()
+        for i in range(2):
+            sibx(o, line, i, 1 - p.core).wait_recv()
+
+    def hop(q, _):
+        z_arrives(p.nth_row(q))
+        y_arrives(p.nth_row(q - 1), range(4))
+        before = p.nth_row(q - 1)
+
+        @pl.when(q > 1)
+        def _():
+            x_arrives(before, 0)
+
+        add_shard(owner(before, 0, p.core))
+
+        @pl.when(q == 1)
         def _():
             advantages()
 
-        @pl.when(s == 2)
-        def _():
-            placement()
-
-        @pl.when(s == 3)
+        @pl.when((q == 2) & p.at_end)
+        def _():
+            @pl.loop(2, L)
+            def _(k):
+                ext_copies(jnp.where(p.row > 0, p.row - k, p.row + k))
+
+        @pl.when(q == 2)
         def _():
             columns()
 
-        @pl.when(s > 1)
-        def _():
-            other = theirs(s - 2)
-            for i in range(4):
-                sibr_copy(other, s - 2, i).wait_recv()
-            for i in range(2):
-                sibx_copy(other, s - 2, i).wait_recv()
-            add_shard(other)
+        @pl.when(q > 1)
+        def _():
+            o = p.nth_row(q - 2)
+            x_arrives(o, 1)
+            add_shard(owner(o, 1, p.core))
+            sib_arrives(o, 0)
+            add_shard(owner(o, 0, 1 - p.core))
+
+        @pl.when(q > 2)
+        def _():
+            o = p.nth_row(q - 3)
+            sib_arrives(o, 1)
+            add_shard(owner(o, 1, 1 - p.core))
 
         return 0
 
-    lax.fori_loop(1, p.ring, hop, 0)
+    lax.fori_loop(1, L, hop, 0)
+
     def term(index, cut):
         rows_at = pl.ds(pl.multiple_of(index * block, block), block)
         return jnp.dot(normed[index], held[rows_at, lanes(*cut)], preferred_element_type=F32)
 
-    def last_x():
-        for i in range(2):
-            x_arrival(mine(last), last, i).wait_recv()
-            sibx_copy(mine(last), last, i).start()
-
-    def await_sibling(s, ring_part, x_part):
-        if ring_part:
-            for i in range(4):
-                sibr_copy(theirs(s), s, i).wait_recv()
-        if x_part:
-            for i in range(2):
-                sibx_copy(theirs(s), s, i).wait_recv()
-
-    await_sibling(last - 1, True, True)
+    far, farther, farthest = p.nth_row(L - 3), p.nth_row(L - 2), p.nth_row(L - 1)
+    sib_arrives(farther, 0)
+    add_shard(owner(farther, 0, 1 - p.core))
+    sib_arrives(far, 1)
+    add_shard(owner(far, 1, 1 - p.core))
+    y_arrives(farthest, (0, 1))
+    x_arrives(farthest, 0)
+    add_shard(owner(farthest, 0, p.core))
+    x_arrives(farther, 1)
+    add_shard(owner(farther, 1, p.core))
+    sib_arrives(farthest, 0)
+    add_shard(owner(farthest, 0, 1 - p.core))
+    sib_arrives(farther, 1)
+    add_shard(owner(farther, 1, 1 - p.core))
+    y_arrives(farthest, (2, 3))
     if whole_blocks:
-        pair = (mine(last), theirs(last))
-        add(theirs(last - 1))
+        pair = (owner(farthest, 1, p.core), owner(farthest, 1, 1 - p.core))
     else:
-        last_x()
-        await_sibling(last, True, True)
+        x_arrives(farthest, 1)
+        sib_arrives(farthest, 1)
         lax.fori_loop(0, width // block - 2, lambda b, _: (add(b), 0)[1], 0)
         pair = (width // block - 2, width // block - 1)
 
@@ -333,21 +388,26 @@
     def same_line(cut):
         row_copy(p.sibling, cut).start()
 
-        @pl.loop(1, L)
-        def _(k):
-            to = lax.rem(p.row + k, L)
-            row_copy(p.at(to, p.col, 0), cut).start()
-            row_copy(p.at(to, p.col, 1), cut).start()
+        @pl.when(jnp.logical_not(p.at_end))
+        def _():
+            @pl.loop(1, L)
+            def _(k):
+                to = lax.rem(p.row + k, L)
+                row_copy(p.at(to, p.col, 0), cut).start()
+                row_copy(p.at(to, p.col, 1), cut).start()
 
     def other_line(m, cut):
         to = lax.rem(p.row + L // 2 + m, L)
-        row_copy(p.at(to, 1 - p.col, 0), cut).start()
-        row_copy(p.at(to, 1 - p.col, 1), cut).start()
+
+        @pl.when(jnp.logical_not(p.at_end) | (to == p.row))
+        def _():
+            row_copy(p.at(to, 1 - p.col, 0), cut).start()
+            row_copy(p.at(to, 1 - p.col, 1), cut).start()
 
     square = jnp.zeros((rows, LANES), F32)
     for i, cut in enumerate(ring_cuts):
         if whole_blocks:
-            sibr_copy(theirs(last), last, i).wait_recv()
+            sibr(farthest, 1, i, 1 - p.core).wait_recv()
         square = finish(cut, square)
 
     @pl.loop(0, L - 1)
@@ -356,10 +416,10 @@
 
     same_line(ring_part)
     if whole_blocks:
-        last_x()
+        x_arrives(farthest, 1)
     for i, cut in enumerate(x_cuts):
         if whole_blocks:
-            sibx_copy(theirs(last), last, i).wait_recv()
+            sibx(farthest, 1, i, 1 - p.core).wait_recv()
         square = finish(cut, square)
     same_line(x_part)
     stay = pltpu.make_async_copy(send.at[me], hid_ref.at[me], load_sems.at[2])
@@ -408,78 +468,94 @@
         g = jnp.dot(gscaled, headb[:, j * tile : (j + 1) * tile], preferred_element_type=F32)
         ghid[:, cut] = (g - hidden[:, cut] * pull).astype(BF16)
 
-    def product(owner, cut):
-        index = owner if whole_blocks else owner * shard // block
-        value = lax.dot_general(
-            normed[index], ghid[:, cut], (((0,), (0,)), ((), ())), preferred_element_type=F32
-        )
-        if whole_blocks:
-            return value
-        prod[...] = value
-        return prod[pl.ds(pl.multiple_of(lax.rem(owner * shard, block), shard), shard)]
+    turns = 2 * jnp.minimum(p.row, L - 1 - p.row)
+    up_first = 2 * p.row < L
 
     def goes_up(k):
-        up_first = 2 * p.row < L
-        return jnp.where(up_first, k < L - 1 - p.row, (k >= p.row) & (k < L - 1))
+        first = (k >= turns) | (lax.rem(k, 2) == 0)
+        return (k < L - 1) & (first == up_first)
 
     def target(k):
-        ups, downs = L - 1 - p.row, p.row
-        up_first = 2 * p.row < L
-        up_at = jnp.where(up_first, k, k - downs)
-        down_at = jnp.where(up_first, k - ups, k)
-        up = goes_up(k)
-        return jnp.where(up, L - 1 - up_at, jnp.where(k < L - 1, down_at, p.row))
+        at = jnp.where(k < turns, k // 2, k - turns // 2)
+        return jnp.where(goes_up(k), L - 1 - at, jnp.where(k < L - 1, at, p.row))
+
+    zw = zq_in.shape[3]
+    yw = width - zw
+    y_cuts = [pl.ds(*c) for c in cuts_of(0, yw, 3)]
+    z_cuts = [pl.ds(*c) for c in cuts_of(yw, zw, 2)]
+    z_local = [pl.ds(*c) for c in cuts_of(0, zw, 2)]
+    ny = len(y_cuts)
 
     def sib_copy(slot, j):
+        cut = (y_cuts + z_cuts)[j]
         return remote(
-            sib_out.at[slot, :, tiles[j]], sib_in.at[slot, :, tiles[j]], rs_sib_send, rs_sib_recv.at[slot, j], sibling
+            sib_out.at[slot, :, cut], sib_in.at[slot, :, cut], rs_sib_send, rs_sib_recv.at[slot, j], sibling
         )
 
     def y_copy(k, j):
         return remote(
-            y_out.at[k, :, tiles[j]], y_in.at[k, :, tiles[j]], y_send, y_recv.at[k, j],
-            {"fsdp": p.at(p.row, 1 - p.col, p.core)},
+            y_out.at[k, :, y_cuts[j]], y_in.at[k, :, y_cuts[j]], y_send, y_recv.at[k, j], across
         )
 
-    def for_sibling(k, cross):
-        slot = 2 * k + cross
-        owner = p.at(target(k), (1 - p.col) if cross else p.col, 1 - p.core)
-        for j, cut in enumerate(tiles):
-            sib_out[slot, :, cut] = product(owner, cut).astype(BF16)
-            sib_copy(slot, j).start()
-
-    def for_me(k, cross):
-        owner = p.at(target(k), (1 - p.col) if cross else p.col, p.core)
-        for cut in tiles:
-            own[k, :, cut] = product(owner, cut)
-
-    def send_y(k):
-        for_sibling(k, 1)
-        for_me(k, 1)
-        for j, cut in enumerate(tiles):
+    def yq_copy(j):
+        return remote(yq_out.at[:, z_local[j]], yq_in.at[:, z_local[j]], yq_send, yq_recv.at[j], across)
+
+    def contribute(k):
+        rows_at = pl.ds(pl.multiple_of(target(k) * 4 * shard, 4 * shard), 4 * shard)
+
+        def share(cross, core):
+            line = (1 - p.col) if cross else p.col
+            return pl.ds(pl.multiple_of((line * 2 + core) * shard, shard), shard)
+
+        for j, cut in enumerate(y_cuts + z_cuts):
+            layer[:, cut] = jnp.dot(normed_t[rows_at], ghid[:, cut], preferred_element_type=F32)
+            for cross in (1, 0):
+                sib_out[2 * k + cross, :, cut] = layer[share(cross, 1 - p.core), cut].astype(BF16)
+                sib_copy(2 * k + cross, j).start()
+        for cut in y_cuts:
+            own[k, :, cut] = layer[share(0, p.core), cut]
+        for cross in (1, 0):
+            for cut, at in zip(z_cuts, z_local):
+                ownz[k, cross, :, at] = layer[share(cross, p.core), cut]
+        for j, cut in enumerate(y_cuts):
             sib_copy(2 * k + 1, j).wait_recv()
-            y_out[k, :, cut] = (own[k, :, cut] + sib_in[2 * k + 1, :, cut].astype(F32)).astype(BF16)
+            y_out[k, :, cut] = (
+                layer[share(1, p.core), cut] + sib_in[2 * k + 1, :, cut].astype(F32)
+            ).astype(BF16)
             y_copy(k, j).start()
 
     def chip_sum(k, j):
-        cut = tiles[j]
+        cut = y_cuts[j]
         sib_copy(2 * k, j).wait_recv()
         y_copy(k, j).wait_recv()
         return own[k, :, cut] + sib_in[2 * k, :, cut].astype(F32) + y_in[k, :, cut].astype(F32)
 
+    def line_sum(k, j):
+        for cross in range(2):
+            sib_copy(2 * k + cross, ny + j).wait_recv()
+            ownz[k, cross, :, z_local[j]] += sib_in[2 * k + cross, :, z_cuts[j]].astype(F32)
+
+    def line_add(k, slot, j):
+        zq_copy(0, slot, 0, j).wait_recv()
+        for cross in range(2):
+            ownz[k, cross, :, z_local[j]] += zq_in[slot, cross, :, z_local[j]].astype(F32)
+
+    def zq_copy(to, slot, k, j):
+        return remote(
+            zq_out.at[k, :, :, z_local[j]], zq_in.at[slot, :, :, z_local[j]], zq_send, zq_recv.at[slot, j],
+            {"fsdp": p.at(to, p.col, p.core)},
+        )
+
     def z_copy(to, slot, k, j):
         return remote(
-            z_out.at[k, :, tiles[j]], z_in.at[slot, :, tiles[j]], z_send, z_recv.at[slot, j],
+            z_out.at[k, :, y_cuts[j]], z_in.at[slot, :, y_cuts[j]], z_send, z_recv.at[slot, j],
             {"fsdp": p.at(to, p.col, p.core)},
         )
 
     def z_arrival(slot, j):
-        return remote(
-            z_out.at[0, :, tiles[j]], z_in.at[slot, :, tiles[j]], z_send, z_recv.at[slot, j],
-            {"fsdp": p.sibling},
-        )
-
-    send_y(0)
+        return z_copy(0, slot, 0, j)
+
+    contribute(0)
     other_line(0, x_part)
 
     gparts = two_parts(ghead)
@@ -515,33 +591,74 @@
 
         when_reducer(go)
 
-    def first_stage(k, _):
-        @pl.when(k == 1)
-        def _():
-            other_line(L - 1, ring_part)
-
-        other_line(k, x_part)
-        send_y(k)
-        return 0
-
-    lax.fori_loop(1, L, first_stage, 0)
-
-    def second_stage(k, _):
-        for_sibling(k, 0)
-        for_me(k, 0)
-        return 0
-
-    lax.fori_loop(0, L, second_stage, 0)
-
-    def third_stage(k, _):
-        t = target(k)
+    def chain(k):
         up = goes_up(k)
         has_in = jnp.where(up, p.row > 0, p.row < L - 1)
         to = jnp.where(up, p.row + 1, p.row - 1)
-        slot = jnp.where((t == to) & jnp.logical_not(up), L, t)
-        for j, cut in enumerate(tiles):
-            total = chip_sum(k, j)
-            own[k, :, cut] = total
+        slot = jnp.where((target(k) == to) & jnp.logical_not(up), L, target(k))
+        return has_in, to, slot
+
+    def whole_line(k):
+        has_in, to, slot = chain(k)
+        for j, at in enumerate(z_local):
+            line_sum(k, j)
+
+            @pl.when(has_in)
+            def _():
+                line_add(k, target(k), j)
+
+            for cross in range(2):
+                zq_out[k, cross, :, at] = ownz[k, cross, :, at].astype(BF16)
+            zq_copy(to, slot, k, j).start()
+
+    @pl.when(p.at_end)
+    def _():
+        whole_line(0)
+
+    n_ext = ext_in.shape[0]
+    rows_e = n_ext * slot_rows
+
+    def early_rows():
+        @pl.when(p.at_end)
+        def _():
+            await_bytes(ext_in.at[pl.ds(0, n_ext // 2)], ext_recv)
+
+        @pl.when(jnp.logical_not(p.at_end))
+        def _():
+            await_bytes(ext_in, ext_recv)
+
+        def early(cut):
+            return ext_in[:, :, cut].astype(F32).reshape(rows_e, cut.size)
+
+        square_e = jnp.zeros((rows_e, LANES), F32)
+        for j in range(0, width, LANES):
+            xf = early(pl.ds(j, LANES))
+            square_e = square_e + xf * xf
+        scale_e = lax.rsqrt(jnp.sum(square_e, -1, keepdims=True) / width + NORM_EPS)
+        for cut in tiles:
+            normed_e[:, cut] = (early(cut) * scale_e * gain_ref[:, cut]).astype(BF16)
+        for cut in tiles:
+            h = early(cut) + jnp.dot(normed_e[...], held[:, cut], preferred_element_type=F32)
+            ext_out[:, :, cut] = h.astype(BF16).reshape(n_ext, slot_rows, tile)
+        for end in range(2):
+            @pl.when(p.row != end * (L - 1))
+            def _():
+                for core in range(2):
+                    source = p.at(end * (L - 1), p.col, core)
+                    slot = (end * 2 + core) * 2
+                    hid_ref[source] = ext_out[slot]
+                    remote(ext_out.at[slot + 1], hid_ref.at[source], fwd_send, a2a_recv, across).start()
+
+    def pass_on(k):
+        t = target(k)
+        has_in, to, slot = chain(k)
+
+        @pl.when(jnp.logical_not(p.at_end))
+        def _():
+            whole_line(k)
+
+        for j, cut in enumerate(y_cuts):
+            own[k, :, cut] = chip_sum(k, j)
 
             @pl.when(has_in)
             def _():
@@ -555,10 +672,50 @@
         def _():
             reduce_heads()
 
+    def rest_of(k, _):
+        @pl.when(k == 1)
+        def _():
+            other_line(L - 1, ring_part)
+
+        other_line(k, x_part)
+        contribute(k)
+
+        @pl.when(p.at_end & (k < L - 1))
+        def _():
+            whole_line(k)
+
+        @pl.when(k == min(2, L - 1))
+        def _():
+            early_rows()
+
+        ready = jnp.where(p.at_end, k - 1, k - 2)
+
+        @pl.when(ready >= 0)
+        def _():
+            pass_on(ready)
+
         return 0
 
-    lax.fori_loop(0, L - 1, third_stage, 0)
-    for j, cut in enumerate(tiles):
+    lax.fori_loop(1, L, rest_of, 0)
+
+    @pl.when(jnp.logical_not(p.at_end))
+    def _():
+        pass_on(L - 2)
+
+    for j, at in enumerate(z_local):
+        line_sum(L - 1, j)
+
+        @pl.when(p.row > 0)
+        def _():
+            line_add(L - 1, p.row, j)
+
+        @pl.when(p.row < L - 1)
+        def _():
+            line_add(L - 1, L, j)
+
+        yq_out[:, at] = ownz[L - 1, 1, :, at].astype(BF16)
+        yq_copy(j).start()
+    for j, cut in enumerate(y_cuts):
         grad_ref[:, cut] = chip_sum(L - 1, j)
 
         @pl.when(p.row > 0)
@@ -570,6 +727,10 @@
         def _():
             z_arrival(L, j).wait_recv()
             grad_ref[:, cut] += z_in[L, :, cut].astype(F32)
+
+    for j, (cut, at) in enumerate(zip(z_cuts, z_local)):
+        yq_copy(j).wait_recv()
+        grad_ref[:, cut] = ownz[L - 1, 0, :, at] + yq_in[:, at].astype(F32)
 
     if nb == n:
         await_bytes(head_all.at[pl.ds(0, nb - 1)], head_sems.at[3])
@@ -585,12 +746,26 @@
     for j in range(nb):
         headg_ref[:, j * LANES : (j + 1) * LANES] = head_all[j, 0 : nact + 1, :]
     stdg_ref[...] = head_all[0, nact + 1 : nact + 2, 0:nact]
-    await_bytes(hid_ref.at[pl.ds(0, n - 1)], a2a_recv)
     stay.wait()
-    await_bytes(send.at[pl.ds(0, n - 1)], a2a_send)
-    await_bytes(held.at[pl.ds(0, last * shard), pl.ds(0, width - xw)], ring_send)
-    await_bytes(held.at[pl.ds(0, last * shard), pl.ds(0, xw)], x_send)
-    await_bytes(held.at[pl.ds(0, p.ring * shard)], sib_send)
+
+    @pl.when(p.at_end)
+    def _():
+        await_bytes(hid_ref.at[pl.ds(0, n - 3)], a2a_recv)
+        await_bytes(send.at[pl.ds(0, 3)], a2a_send)
+        await_bytes(ext_out.at[pl.ds(0, 2)], fwd_send)
+        await_bytes(obs_send.at[pl.ds(0, 4 * (L - 1))], ext_send)
+        await_bytes(held.at[pl.ds(0, shard), pl.ds(0, width - xw)], z_ag_send)
+
+    @pl.when(jnp.logical_not(p.at_end))
+    def _():
+        await_bytes(hid_ref.at[pl.ds(0, n - 5)], a2a_recv)
+        await_bytes(send.at[pl.ds(0, n - 1)], a2a_send)
+        await_bytes(ext_out.at[pl.ds(0, 4)], fwd_send)
+        await_bytes(held.at[pl.ds(0, (L + 1) * shard), pl.ds(0, width - xw)], z_ag_send)
+
+    await_bytes(held.at[pl.ds(0, L * shard), pl.ds(0, width - xw)], y_ag_send)
+    await_bytes(held.at[pl.ds(0, (2 * L - 1) * shard), pl.ds(0, xw)], x_send)
+    await_bytes(held.at[pl.ds(0, 2 * L * shard)], sib_send)
     await_bytes(stats.at[pl.ds(0, n - 1)], stat_send)
     if nb == n:
         await_bytes(head_blk.at[pl.ds(0, nb - 1)], head_sems.at[0])
@@ -608,6 +783,8 @@
     await_bytes(sib_out, rs_sib_send)
     await_bytes(y_out, y_send)
     await_bytes(z_out.at[pl.ds(0, L - 1)], z_send)
+    await_bytes(zq_out.at[pl.ds(0, L - 1)], zq_send)
+    await_bytes(yq_out, yq_send)
 
 
 def store_kernel(a, b, c, d, a_out, b_out, c_out, d_out, sems):
@@ -634,8 +811,9 @@
     per = rows // n
     slot_rows = -(-per // 8) * 8
     L = n // 4
-    ring = n // 2
     nb = min(n, width // LANES)
+    zw = width // LANES * 4 // 16 * LANES
+    yw = width - zw
     vmem = pl.BlockSpec(memory_space=pltpu.VMEM)
     hbm = pl.BlockSpec(memory_space=pl.ANY)
     sem = pltpu.SemaphoreType.DMA
@@ -673,19 +851,34 @@
             V((nb, 16, LANES), F32),
             V((2 * L, shard, width), BF16),
             V((2 * L, shard, width), BF16),
-            V((L, shard, width), BF16),
-            V((L, shard, width), BF16),
-            V((L, shard, width), BF16),
-            V((L + 1, shard, width), BF16),
-            V((L, shard, width), F32),
-            V((block, width // 4), F32),
+            V((L, shard, yw), BF16),
+            V((L, shard, yw), BF16),
+            V((L, shard, yw), BF16),
+            V((L + 1, shard, yw), BF16),
+            V((L, 2, shard, zw), BF16),
+            V((L + 1, 2, shard, zw), BF16),
+            V((shard, zw), BF16),
+            V((shard, zw), BF16),
+            V((L, shard, yw), F32),
+            V((L, 2, shard, zw), F32),
+            V((width, rows), BF16),
+            V((4 * shard, width), F32),
+            V((n, slot_rows, width), BF16),
+            V((8, slot_rows, width), BF16),
+            V((8, slot_rows, width), BF16),
+            V((8 * slot_rows, width), BF16),
             sem((3,)),
             sem(()),
-            sem((ring, 4)),
-            sem(()),
-            sem((ring, 2)),
-            sem((ring, 4)),
-            sem((ring, 2)),
+            sem((L, 4)),
+            sem(()),
+            sem((L, 4)),
+            sem(()),
+            sem((2 * L, 2)),
+            sem((2 * L, 4)),
+            sem((2 * L, 2)),
+            sem(()),
+            sem(()),
+            sem(()),
             sem(()),
             sem(()),
             sem(()),
@@ -693,14 +886,18 @@
             sem(()),
             sem((4,)),
             sem(()),
-            sem((2 * L, 4)),
-            sem(()),
-            sem((L, 4)),
-            sem(()),
-            sem((L + 1, 4)),
+            sem((2 * L, 5)),
+            sem(()),
+            sem((L, 3)),
+            sem(()),
+            sem((L + 1, 3)),
+            sem(()),
+            sem((L + 1, 2)),
+            sem(()),
+            sem((2,)),
         ],
         compiler_params=pltpu.CompilerParams(
-            collective_id=0, has_side_effects=True, vmem_limit_bytes=54 << 20
+            collective_id=0, has_side_effects=True, vmem_limit_bytes=58 << 20
         ),
         cost_estimate=pl.CostEstimate(
             flops=4 * rows * width * width, bytes_accessed=16 * rows * width, transcendentals=0

time: 113 us -> 108 us (0.956)
  Pallas kernels: 112 us -> 107 us
    pallas_call x1, Pallas kernels: 110 us -> 106 us  [local(): pl.pallas_call(functools.partial(kernel, n, steps), name='step', out_shap...]
where the time goes in v4:
time: 108 us
  Pallas kernels  107 us (99%)
    pallas_call x1, Pallas kernels, local(): pl.pallas_call(functools.partial(kernel, n, steps), name='step', out_shap...  106 us

profile of v4, /device:TPU:0, one launch (start us, length us, event | category | flops | bytes accessed | tf_op | source)
XLA Modules:
  0.0 108.1 jit_solution(15077463837359213003)
XLA Ops:
  0.6 105.7 %step.1 = (bf16[16,24,2048]{2,1,0:T(8,128)(2,1)S(1)}, f32[128,2048]{1,0:T(8,128)S(1)}, f32[13,2048]{1,0:T(8,128)S(1)}, f32[1,12]{1,0:T(1,128)S(1)}) custom-call(bf16[384,2048]{1,0:T(8,128)(2,1)} %x_hbm.1, bf16[128,2048]{1,0:T(8,128)(2,1)} %w_hbm.1, f32[1,2048]{1,0:T(1,128)} %bitcast.13, f32[16,24]{1,0:T(8,128)} %reward_ref.1, f32[16,25]{1,0:T(8,128)} %value_ref.1, ...), custom_call_target="tpu_custom_call" | custom-call | flops 6442450944 | bytes 12582912 | tf_op jit(solution)/shard_map/step/pallas_call | solution.py:821
  106.4 1.6 %store.1 = (bf16[16,24,2048]{2,1,0:T(8,128)(2,1)}, f32[128,2048]{1,0:T(8,128)}, f32[13,2048]{1,0:T(8,128)}, f32[1,12]{1,0:T(1,128)}) custom-call(bf16[16,24,2048]{2,1,0:T(8,128)(2,1)S(1)} %get-tuple-element.12.a, f32[128,2048]{1,0:T(8,128)S(1)} %get-tuple-element.13.b, f32[13,2048]{1,0:T(8,128)S(1)} %get-tuple-element.14.c, f32[1,12]{1,0:T(1,128)S(1)} %get-tuple-element.15.d), custom_call_target="tpu_custom_call" | custom-call | tf_op jit(solution)/shard_map/store/pallas_call | solution.py:910

commit v5 on v4

--- a/solution.py
+++ b/solution.py
@@ -312,11 +312,9 @@
         def _():
             advantages()
 
-        @pl.when((q == 2) & p.at_end)
-        def _():
-            @pl.loop(2, L)
-            def _(k):
-                ext_copies(jnp.where(p.row > 0, p.row - k, p.row + k))
+        @pl.when((q > 1) & p.at_end)
+        def _():
+            ext_copies(jnp.where(p.row > 0, p.row - q, p.row + q))
 
         @pl.when(q == 2)
         def _():
@@ -410,7 +408,7 @@
             sibr(farthest, 1, i, 1 - p.core).wait_recv()
         square = finish(cut, square)
 
-    @pl.loop(0, L - 1)
+    @pl.loop(0, L)
     def _(m):
         other_line(m, ring_part)
 
@@ -421,6 +419,10 @@
         if whole_blocks:
             sibx(farthest, 1, i, 1 - p.core).wait_recv()
         square = finish(cut, square)
+    @pl.loop(0, L)
+    def _(m):
+        other_line(m, x_part)
+
     same_line(x_part)
     stay = pltpu.make_async_copy(send.at[me], hid_ref.at[me], load_sems.at[2])
     stay.start()
@@ -512,17 +514,17 @@
             for cross in (1, 0):
                 sib_out[2 * k + cross, :, cut] = layer[share(cross, 1 - p.core), cut].astype(BF16)
                 sib_copy(2 * k + cross, j).start()
-        for cut in y_cuts:
-            own[k, :, cut] = layer[share(0, p.core), cut]
-        for cross in (1, 0):
-            for cut, at in zip(z_cuts, z_local):
-                ownz[k, cross, :, at] = layer[share(cross, p.core), cut]
         for j, cut in enumerate(y_cuts):
             sib_copy(2 * k + 1, j).wait_recv()
             y_out[k, :, cut] = (
                 layer[share(1, p.core), cut] + sib_in[2 * k + 1, :, cut].astype(F32)
             ).astype(BF16)
             y_copy(k, j).start()
+        for cut in y_cuts:
+            own[k, :, cut] = layer[share(0, p.core), cut]
+        for cross in (1, 0):
+            for cut, at in zip(z_cuts, z_local):
+                ownz[k, cross, :, at] = layer[share(cross, p.core), cut]
 
     def chip_sum(k, j):
         cut = y_cuts[j]
@@ -556,7 +558,6 @@
         return z_copy(0, slot, 0, j)
 
     contribute(0)
-    other_line(0, x_part)
 
     gparts = two_parts(ghead)
     row = lax.broadcasted_iota(jnp.int32, (16, LANES), 0)
@@ -673,11 +674,6 @@
             reduce_heads()
 
     def rest_of(k, _):
-        @pl.when(k == 1)
-        def _():
-            other_line(L - 1, ring_part)
-
-        other_line(k, x_part)
         contribute(k)
 
         @pl.when(p.at_end & (k < L - 1))

time: 108 us -> 107 us (level)
    pallas_call x1, Pallas kernels: 106 us -> 104 us  [local(): pl.pallas_call(functools.partial(kernel, n, steps), name='step', out_shap...]
where the time goes in v5:
time: 107 us
  Pallas kernels  106 us (99%)
    pallas_call x1, Pallas kernels, local(): pl.pallas_call(functools.partial(kernel, n, steps), name='step', out_shap...  104 us

profile of v5, /device:TPU:0, one launch (start us, length us, event | category | flops | bytes accessed | tf_op | source)
XLA Modules:
  0.0 106.8 jit_solution(2482462919874176710)
XLA Ops:
  0.6 104.5 %step.1 = (bf16[16,24,2048]{2,1,0:T(8,128)(2,1)S(1)}, f32[128,2048]{1,0:T(8,128)S(1)}, f32[13,2048]{1,0:T(8,128)S(1)}, f32[1,12]{1,0:T(1,128)S(1)}) custom-call(bf16[384,2048]{1,0:T(8,128)(2,1)} %x_hbm.1, bf16[128,2048]{1,0:T(8,128)(2,1)} %w_hbm.1, f32[1,2048]{1,0:T(1,128)} %bitcast.13, f32[16,24]{1,0:T(8,128)} %reward_ref.1, f32[16,25]{1,0:T(8,128)} %value_ref.1, ...), custom_call_target="tpu_custom_call" | custom-call | flops 6442450944 | bytes 12582912 | tf_op jit(solution)/shard_map/step/pallas_call | solution.py:817
  105.1 1.6 %store.1 = (bf16[16,24,2048]{2,1,0:T(8,128)(2,1)}, f32[128,2048]{1,0:T(8,128)}, f32[13,2048]{1,0:T(8,128)}, f32[1,12]{1,0:T(1,128)}) custom-call(bf16[16,24,2048]{2,1,0:T(8,128)(2,1)S(1)} %get-tuple-element.12.a, f32[128,2048]{1,0:T(8,128)S(1)} %get-tuple-element.13.b, f32[13,2048]{1,0:T(8,128)S(1)} %get-tuple-element.14.c, f32[1,12]{1,0:T(1,128)S(1)} %get-tuple-element.15.d), custom_call_target="tpu_custom_call" | custom-call | tf_op jit(solution)/shard_map/store/pallas_call | solution.py:906

commit v6 on v5

--- a/solution.py
+++ b/solution.py
@@ -419,10 +419,6 @@
         if whole_blocks:
             sibx(farthest, 1, i, 1 - p.core).wait_recv()
         square = finish(cut, square)
-    @pl.loop(0, L)
-    def _(m):
-        other_line(m, x_part)
-
     same_line(x_part)
     stay = pltpu.make_async_copy(send.at[me], hid_ref.at[me], load_sems.at[2])
     stay.start()
@@ -558,6 +554,11 @@
         return z_copy(0, slot, 0, j)
 
     contribute(0)
+
+    @pl.loop(0, L)
+    def _(m):
+        other_line(m, x_part)
+
 
     gparts = two_parts(ghead)
     row = lax.broadcasted_iota(jnp.int32, (16, LANES), 0)

time: 107 us -> 107 us (level)
  no operation moved by 1% of the time
where the time goes in v6:
time: 107 us
  Pallas kernels  106 us (99%)
    pallas_call x1, Pallas kernels, local(): pl.pallas_call(functools.partial(kernel, n, steps), name='step', out_shap...  104 us

profile of v6, /device:TPU:0, one launch (start us, length us, event | category | flops | bytes accessed | tf_op | source)
XLA Modules:
  0.0 106.8 jit_solution(7082015713243319508)
XLA Ops:
  0.6 104.5 %step.1 = (bf16[16,24,2048]{2,1,0:T(8,128)(2,1)S(1)}, f32[128,2048]{1,0:T(8,128)S(1)}, f32[13,2048]{1,0:T(8,128)S(1)}, f32[1,12]{1,0:T(1,128)S(1)}) custom-call(bf16[384,2048]{1,0:T(8,128)(2,1)} %x_hbm.1, bf16[128,2048]{1,0:T(8,128)(2,1)} %w_hbm.1, f32[1,2048]{1,0:T(1,128)} %bitcast.13, f32[16,24]{1,0:T(8,128)} %reward_ref.1, f32[16,25]{1,0:T(8,128)} %value_ref.1, ...), custom_call_target="tpu_custom_call" | custom-call | flops 6442450944 | bytes 12582912 | tf_op jit(solution)/shard_map/step/pallas_call | solution.py:818
  105.1 1.6 %store.1 = (bf16[16,24,2048]{2,1,0:T(8,128)(2,1)}, f32[128,2048]{1,0:T(8,128)}, f32[13,2048]{1,0:T(8,128)}, f32[1,12]{1,0:T(1,128)}) custom-call(bf16[16,24,2048]{2,1,0:T(8,128)(2,1)S(1)} %get-tuple-element.12.a, f32[128,2048]{1,0:T(8,128)S(1)} %get-tuple-element.13.b, f32[13,2048]{1,0:T(8,128)S(1)} %get-tuple-element.14.c, f32[1,12]{1,0:T(1,128)S(1)} %get-tuple-element.15.d), custom_call_target="tpu_custom_call" | custom-call | tf_op jit(solution)/shard_map/store/pallas_call | solution.py:907
